TPU v7x, 128 devices: a whole 4x4x4 slice. The times are simulated.
128 devices in a mesh: rows: 16 (over z, x), cents: 8 (over y, core).
Axes of the slice: x: 4, y: 4, z: 4, core: 2. Of those that a mesh axis runs over, the one named last changes fastest.
Arguments:
- groups: bfloat16 [262144, 1024], P(('rows', 'cents')), may hold values from -60 to 60
- centroids: bfloat16 [262144, 1024], P(('rows', 'cents')), may hold values from -60 to 60
- row_weight: float32 [262144], P(('rows', 'cents')), may hold values from 0.5 to 18
- block_ids: int32 [1024, 8], P(('rows', 'cents')), may hold values from 0 to 2047, as said below
- block_counts: int32 [1024], P(('rows', 'cents')), may hold values from 1 to 8
Outputs:
- centroid_sums: float32 [262144, 1024], P(('rows', 'cents'))
- column_load: float32 [262144], P(('rows', 'cents'))
Inputs may be any that keep to these rules, and one draw needn't show every extreme that they name: `block_ids`: slots k < block_counts[b] are the candidates of row block b; later slots hold valid ids but are unused. List block g is held by the device of index g // 16 in the order rows, then cents. The 8 x 8 slots of the row blocks held by device (r, c) name blocks held by devices (o, c) only, exactly 4 slots for each o, and among those slots exactly 2 distinct blocks of o; the slots of one row block name blocks of distinct holders.
All inputs are finite; a program needn't handle non-finite values.
Results may differ from a plain program's by a relative error of at most 0.0051.
Values may be sent and summed in bfloat16 or wider, within the bound.
No kernel may reach another device: no remote copies, remote signals or barrier semaphores. Data moves between devices by JAX's collectives and lax.ppermute only.
A program may use at most 192 MiB of HBM per device.

v0:
```python
import jax
import jax.numpy as jnp
from jax import lax
from jax.sharding import PartitionSpec as P

D = 1024
RB = 256
CB = 128
USE = 2
ITERS = 3


BETA = 32.0
EPSILON = 1e-06
PRIOR = 0.25
HIGHEST = lax.Precision.HIGHEST


def normalize(values):
    widened = values.astype(jnp.float32)
    factor = lax.rsqrt(jnp.mean(widened * widened, axis=-1, keepdims=True) + EPSILON)
    return (widened * factor).astype(jnp.bfloat16)


def routing(block_ids, lists_blocks, cents_count, rows_count, use_count):
    block_total, slots_per_block = block_ids.shape
    pair_count = block_total * slots_per_block
    flat_ids = block_ids.reshape(pair_count)
    holder_row = flat_ids // lists_blocks // cents_count
    local_block = flat_ids % lists_blocks
    pair_index = jnp.arange(pair_count, dtype=jnp.int32)
    same_id = flat_ids[None, :] == flat_ids[:, None]
    first_pair = jnp.min(jnp.where(same_id, pair_index[None, :], pair_count), axis=1)
    is_first = first_pair == pair_index
    earlier_first = (
        is_first[None, :]
        & (holder_row[None, :] == holder_row[:, None])
        & (pair_index[None, :] < pair_index[:, None])
    )
    rank_first = jnp.sum(earlier_first.astype(jnp.int32), axis=1)
    distinct_of_pair = holder_row * use_count + rank_first[first_pair]
    distinct_index = jnp.arange(rows_count * use_count, dtype=jnp.int32)
    chosen = (is_first[None, :] & (distinct_of_pair[None, :] == distinct_index[:, None])).astype(
        jnp.int32
    )
    request_table = jnp.sum(chosen * local_block[None, :], axis=1).reshape(rows_count, use_count)
    pair_onehot = (distinct_of_pair[None, :] == distinct_index[:, None]).astype(jnp.float32)
    dense_of_pair = holder_row * lists_blocks + local_block
    return (distinct_of_pair, request_table, pair_onehot, dense_of_pair)


def holder_onehot(local_in, lists_blocks):
    return (
        local_in.reshape(-1)[None, :] == jnp.arange(lists_blocks, dtype=jnp.int32)[:, None]
    ).astype(jnp.float32)


def body(groups, centroids, row_weight, block_ids, block_counts):
    rows_count = lax.axis_size("rows")
    cents_count = lax.axis_size("cents")
    use_count = USE
    block_total, slots_per_block = block_ids.shape
    lists_blocks = centroids.shape[0] // CB
    rows_norm = normalize(groups).reshape(block_total, RB, D)
    lists_norm = normalize(centroids).reshape(lists_blocks, CB, D)
    weights = row_weight.reshape(block_total, RB)
    weight_sum = lax.psum(jnp.sum(row_weight), ("rows", "cents"))
    target = weight_sum / (lists_blocks * CB * rows_count * cents_count)
    distinct_of_pair, request_table, pair_onehot, dense_of_pair = routing(
        block_ids, lists_blocks, cents_count, rows_count, use_count
    )
    local_in = lax.all_to_all(request_table, "rows", split_axis=0, concat_axis=0, tiled=True)
    owned_map = holder_onehot(local_in, lists_blocks)
    arrived = lax.all_to_all(lists_norm[local_in], "rows", split_axis=0, concat_axis=0, tiled=True)
    picked_lists = arrived.reshape(-1, CB, D)[distinct_of_pair].reshape(
        block_total, slots_per_block, CB, D
    )
    scores = jnp.einsum(
        "brd,bkcd->bkrc", rows_norm, picked_lists, preferred_element_type=jnp.float32
    )
    live_mask = (
        jnp.arange(slots_per_block, dtype=jnp.int32)[None, :] < block_counts[:, None]
    ).astype(jnp.float32)
    kernel = jnp.exp(scores * (BETA / D)) * live_mask[:, :, None, None]
    picked = jnp.ones((block_total, slots_per_block, CB), jnp.float32)
    for iteration in range(ITERS):
        row_sums = jnp.einsum("bkrc,bkc->br", kernel, picked, precision=HIGHEST)
        row_scale = weights / row_sums
        column_parts = jnp.einsum("bkrc,br->bkc", kernel, row_scale, precision=HIGHEST)
        flat_parts = column_parts.reshape(-1, CB)
        outgoing = jnp.dot(pair_onehot, flat_parts, precision=HIGHEST).reshape(
            rows_count, use_count, CB
        )
        incoming = lax.all_to_all(outgoing, "rows", split_axis=0, concat_axis=0, tiled=True)
        column = jnp.dot(owned_map, incoming.reshape(-1, CB), precision=HIGHEST)
        scales = target / (column + PRIOR * target)
        returned = lax.all_to_all(scales[local_in], "rows", split_axis=0, concat_axis=0, tiled=True)
        picked = returned.reshape(-1, CB)[distinct_of_pair].reshape(
            block_total, slots_per_block, CB
        )
    row_sums = jnp.einsum("bkrc,bkc->br", kernel, picked, precision=HIGHEST)
    row_scale = weights / row_sums
    transport = row_scale[:, None, :, None] * kernel * picked[:, :, None, :]
    mass_parts = jnp.dot(
        pair_onehot, jnp.sum(transport, axis=2).reshape(-1, CB), precision=HIGHEST
    ).reshape(rows_count, use_count, CB)
    transport_half = transport.astype(jnp.bfloat16)
    slot_target = distinct_of_pair.reshape(block_total, slots_per_block)
    gathered_sums = jnp.zeros((rows_count * use_count, CB, D), jnp.float32)
    for slot_number in range(slots_per_block):
        slot_part = jnp.einsum(
            "brc,brd->bcd",
            transport_half[:, slot_number],
            rows_norm,
            preferred_element_type=jnp.float32,
        )
        gathered_sums = gathered_sums.at[slot_target[:, slot_number]].add(slot_part)
    got_parts, got_mass = (
        lax.all_to_all(
            gathered_sums.reshape(rows_count, use_count, CB, D),
            "rows",
            split_axis=0,
            concat_axis=0,
            tiled=True,
        ),
        lax.all_to_all(mass_parts, "rows", split_axis=0, concat_axis=0, tiled=True),
    )
    totals = jnp.dot(
        owned_map, got_parts.reshape(rows_count * use_count, CB * D), precision=HIGHEST
    )
    column_mass = jnp.dot(owned_map, got_mass.reshape(-1, CB), precision=HIGHEST)
    return (totals.reshape(-1, D), (column_mass / target).reshape(-1))


def solution(mesh):
    placed = (
        P(("rows", "cents"), None),
        P(("rows", "cents"), None),
        P(("rows", "cents")),
        P(("rows", "cents"), None),
        P(("rows", "cents")),
    )
    return jax.shard_map(
        body,
        mesh=mesh,
        in_specs=placed,
        out_specs=(P(("rows", "cents"), None), P(("rows", "cents"))),
        check_vma=False,
    )
```

profile of v0, /device:TPU:0, one launch (start us, length us, event | category | flops | bytes accessed | tf_op | source)
XLA Modules:
  0.0 761.9 jit_solution(4202398245936363238)
XLA Ops:
  3.4 8.0 %all-to-all-start = ((s32[16,1,2]{2,1,0:T(1,128)}), s32[16,1,2]{2,1,0:T(1,128)S(1)}, u32[]{:S(2)}, u32[]{:S(2)}) async-start(s32[16,1,2]{2,1,0:T(1,128)} %bitcast.2), calls=%async_computation | async-start | bytes 16384 | tf_op jit(solution)/shard_map/all_to_all | solution.py:72
  39.1 116.5 %all-to-all-done.1 = bf16[16,2,128,1024]{3,2,1,0:T(8,128)(2,1)} async-done(((bf16[16,2,128,1024]{3,2,1,0:T(8,128)(2,1)}), bf16[16,2,128,1024]{3,2,1,0:T(8,128)(2,1)}, u32[]{:S(2)}, u32[]{:S(2)}) %all-to-all-start.1) | async-done | bytes 8388640 | tf_op jit(solution)/shard_map/all_to_all | solution.py:74
  155.5 11.0 %gather_fusion.2 = bf16[64,128,1024]{2,1,0:T(8,128)(2,1)} fusion(bf16[32,128,1024]{2,1,0:T(8,128)(2,1)} %bitcast.6, s32[1024]{0:T(1024)S(1)} %pad_clamp_fusion), kind=kCustom, calls=%fused_computation.2 | custom fusion | bytes 33554688 | tf_op jit(solution)/shard_map/gather | solution.py:75
  166.5 15.1 %exponential_multiply_fusion = f32[8,8,128,256]{3,2,1,0:T(8,128)} fusion(f32[8,8]{1,0:T(8,128)S(1)} %fusion.78, bf16[8,8,128,1024]{3,2,1,0:T(8,128)(2,1)} %bitcast.180, bf16[8,256,1024,1]{2,1,3,0:T(8,128)(2,1)} %bitcast.167), kind=kOutput, calls=%fused_computation.41 | convolution fusion | flops 4299161600 | bytes 29360384 | tf_op jit(solution)/shard_map/brd,bkcd->bkrc/dot_general | solution.py:78
  181.6 7.8 %fusion.16 = f32[8,1,256,1]{2,1,3,0:T(1,128)S(1)} fusion(f32[8,8,128,1]{2,3,1,0:T(1,128)S(1)} %bitcast.188, f32[8,8,128,256]{3,2,1,0:T(8,128)} %exponential_multiply_fusion), kind=kOutput, calls=%fused_computation.38 | convolution fusion | flops 25165824 | bytes 8429568 | tf_op jit(solution)/shard_map/bkrc,bkc->br/dot_general | solution.py:87
  203.9 65.5 %psum.7 = f32[]{:T(128)} all-reduce(f32[]{:T(128)} %reduce_sum.58), channel_id=1, replica_groups=mesh['rows'=16,'cents'=8] {'rows','cents'}, use_global_device_ids=true, to_apply=%region_6.7 | all-reduce | flops 1 | bytes 8 | tf_op jit(solution)/shard_map/psum | solution.py:67
  272.8 12.6 %all_to_all.57 = f32[16,2,128]{2,1,0:T(2,128)S(1)} all-to-all(f32[16,2,128]{2,1,0:T(2,128)S(1)} %bitcast.189), channel_id=1, replica_groups=mesh['rows'=16,'cents'=8] {'rows'}, dimensions={0} | all-to-all | bytes 32768 | tf_op jit(solution)/shard_map/all_to_all | solution.py:97
  292.7 9.4 %fusion.10 = f32[8,1,8,128]{3,1,2,0:T(1,128)S(1)} fusion(f32[8,8,128,256]{3,2,1,0:T(8,128)} %exponential_multiply_fusion, f32[8,256,1,1]{1,0,2,3:T(8,128)S(1)} %fusion.45), kind=kOutput, calls=%fused_computation.32 | convolution fusion | flops 25165824 | bytes 8429568 | tf_op jit(solution)/shard_map/bkrc,br->bkc/dot_general | solution.py:89
  302.4 10.7 %all_to_all.58 = f32[16,2,128]{2,1,0:T(2,128)S(1)} all-to-all(f32[16,2,128]{2,1,0:T(2,128)S(1)} %copy.26), channel_id=1, replica_groups=mesh['rows'=16,'cents'=8] {'rows'}, dimensions={0} | all-to-all | bytes 32768 | tf_op jit(solution)/shard_map/all_to_all | solution.py:94
  332.7 9.4 %fusion.6 = f32[8,1,8,128]{3,1,2,0:T(1,128)S(1)} fusion(f32[8,8,128,256]{3,2,1,0:T(8,128)} %exponential_multiply_fusion, f32[8,256,1,1]{1,0,2,3:T(8,128)S(1)} %fusion.44), kind=kOutput, calls=%fused_computation.28 | convolution fusion | flops 25165824 | bytes 8429568 | tf_op jit(solution)/shard_map/bkrc,br->bkc/dot_general | solution.py:89
  346.4 7.5 all-to-all-done.6
  407.5 7.9 %broadcast_in_dim.21 = f32[32,128,1024]{2,1,0:T(8,128)} broadcast(f32[]{:T(128)} %constant.70.clone.1), dimensions={} | broadcast | bytes 16777220 | tf_op jit(solution)/shard_map/broadcast_in_dim | solution.py:109
  415.3 9.4 %scatter_fusion = f32[32,128,1024]{2,1,0:T(8,128)} fusion(f32[32,128,1024]{2,1,0:T(8,128)} %broadcast_in_dim.21, s32[8]{0:T(128)S(1)} %get-tuple-element.9, f32[8,128,1024]{2,1,0:T(8,128)} %fusion.32), kind=kCustom, calls=%fused_computation.9 | custom fusion | flops 1048576 | bytes 12582944 | tf_op jit(solution)/shard_map/scatter-add | solution.py:117
  424.7 9.6 %scatter_fusion.1 = f32[32,128,1024]{2,1,0:T(8,128)} fusion(f32[32,128,1024]{2,1,0:T(8,128)} %scatter_fusion, s32[8]{0:T(128)S(1)} %get-tuple-element.8, f32[8,128,1024]{2,1,0:T(8,128)} %fusion.31), kind=kCustom, calls=%fused_computation.10 | custom fusion | flops 1048576 | bytes 12582944 | tf_op jit(solution)/shard_map/scatter-add | solution.py:117
  434.3 9.5 %scatter_fusion.2 = f32[32,128,1024]{2,1,0:T(8,128)} fusion(f32[32,128,1024]{2,1,0:T(8,128)} %scatter_fusion.1, s32[8]{0:T(128)S(1)} %get-tuple-element.7, f32[8,128,1024]{2,1,0:T(8,128)} %fusion.30), kind=kCustom, calls=%fused_computation.11 | custom fusion | flops 1048576 | bytes 12582944 | tf_op jit(solution)/shard_map/scatter-add | solution.py:117
  443.7 9.5 %scatter_fusion.3 = f32[32,128,1024]{2,1,0:T(8,128)} fusion(f32[32,128,1024]{2,1,0:T(8,128)} %scatter_fusion.2, s32[8]{0:T(128)S(1)} %get-tuple-element.6, f32[8,128,1024]{2,1,0:T(8,128)} %fusion.29), kind=kCustom, calls=%fused_computation.12 | custom fusion | flops 1048576 | bytes 12582944 | tf_op jit(solution)/shard_map/scatter-add | solution.py:117
  453.2 9.4 %scatter_fusion.4 = f32[32,128,1024]{2,1,0:T(8,128)} fusion(f32[32,128,1024]{2,1,0:T(8,128)} %scatter_fusion.3, s32[8]{0:T(128)S(1)} %get-tuple-element.5, f32[8,128,1024]{2,1,0:T(8,128)} %fusion.28), kind=kCustom, calls=%fused_computation.13 | custom fusion | flops 1048576 | bytes 12582944 | tf_op jit(solution)/shard_map/scatter-add | solution.py:117
  462.7 9.5 %scatter_fusion.5 = f32[32,128,1024]{2,1,0:T(8,128)} fusion(f32[32,128,1024]{2,1,0:T(8,128)} %scatter_fusion.4, s32[8]{0:T(128)S(1)} %get-tuple-element.4, f32[8,128,1024]{2,1,0:T(8,128)} %fusion.27), kind=kCustom, calls=%fused_computation.14 | custom fusion | flops 1048576 | bytes 12582944 | tf_op jit(solution)/shard_map/scatter-add | solution.py:117
  472.2 9.4 %scatter_fusion.6 = f32[32,128,1024]{2,1,0:T(8,128)} fusion(f32[32,128,1024]{2,1,0:T(8,128)} %scatter_fusion.5, s32[8]{0:T(128)S(1)} %get-tuple-element.3, f32[8,128,1024]{2,1,0:T(8,128)} %fusion.26), kind=kCustom, calls=%fused_computation.15 | custom fusion | flops 1048576 | bytes 12582944 | tf_op jit(solution)/shard_map/scatter-add | solution.py:117
  481.6 9.6 %scatter_fusion.7 = f32[32,128,1024]{2,1,0:T(8,128)} fusion(f32[32,128,1024]{2,1,0:T(8,128)} %scatter_fusion.6, s32[8]{0:T(128)S(1)} %get-tuple-element.2, f32[8,128,1024]{2,1,0:T(8,128)} %fusion.25), kind=kCustom, calls=%fused_computation.16 | custom fusion | flops 1048576 | bytes 12582944 | tf_op jit(solution)/shard_map/scatter-add | solution.py:117
  491.2 7.6 all-to-all-start.8
  499.5 232.5 %all-to-all-done.8 = f32[16,2,128,1024]{3,2,1,0:T(8,128)} async-done(((f32[16,2,128,1024]{3,2,1,0:T(8,128)}), f32[16,2,128,1024]{3,2,1,0:T(8,128)}, u32[]{:S(2)}, u32[]{:S(2)}) %all-to-all-start.8) | async-done | bytes 16777248 | tf_op jit(solution)/shard_map/all_to_all | solution.py:119
  732.0 15.2 %copy.44 = f32[4,8,128,1024]{3,1,2,0:T(8,128)S(1)} copy(f32[4,8,128,1024]{3,2,1,0:T(8,128)} %bitcast.82) | data formatting | bytes 33554432
  747.2 8.1 %fusion.58 = f32[16,131072]{1,0:T(8,128)} fusion(f32[32,131072]{1,0:T(8,128)S(1)} %bitcast.177, s32[32]{0:T(128)S(1)} %eq.106), kind=kOutput, calls=%fused_computation.113 | convolution fusion | flops 805306880 | bytes 25165952 | tf_op jit(solution)/shard_map/dot_general | solution.py:128
  (100 shorter events, 138.8 us)
Async XLA Ops:
  3.4 15.5 %all-to-all-start = ((s32[16,1,2]{2,1,0:T(1,128)}), s32[16,1,2]{2,1,0:T(1,128)S(1)}, u32[]{:S(2)}, u32[]{:S(2)}) async-start(s32[16,1,2]{2,1,0:T(1,128)} %bitcast.2), calls=%async_computation | async-start | bytes 16384 | tf_op jit(solution)/shard_map/all_to_all | solution.py:72
  11.4 3.5 copy-start.3
  26.6 6.2 copy-start.5
  26.6 6.3 copy-start.6
  26.6 6.4 copy-start.7
  26.6 129.0 %all-to-all-start.1 = ((bf16[16,2,128,1024]{3,2,1,0:T(8,128)(2,1)}), bf16[16,2,128,1024]{3,2,1,0:T(8,128)(2,1)}, u32[]{:S(2)}, u32[]{:S(2)}) async-start(bf16[16,2,128,1024]{3,2,1,0:T(8,128)(2,1)} %bitcast.179), calls=%async_computation.1 | async-start | bytes 16777216 | tf_op jit(solution)/shard_map/all_to_all | solution.py:74
  32.9 3.5 copy-start.4
  181.6 7.8 %copy-start.1 = (f32[8,8,128,256]{3,2,1,0:T(8,128)S(1)}, f32[8,8,128,256]{3,2,1,0:T(8,128)}, u32[]{:S(2)}) copy-start(f32[8,8,128,256]{3,2,1,0:T(8,128)} %exponential_multiply_fusion) | copy-start | bytes 25165828
  197.4 74.6 %all-to-all-start.2 = ((f32[16,2,128]{2,1,0:T(2,128)}), f32[16,2,128]{2,1,0:T(2,128)S(1)}, u32[]{:S(2)}, u32[]{:S(2)}) async-start(f32[16,2,128]{2,1,0:T(2,128)} %copy.25), calls=%async_computation.2 | async-start | bytes 32768 | tf_op jit(solution)/shard_map/all_to_all | solution.py:94
  314.3 11.0 %all-to-all-start.5 = ((f32[16,2,128]{2,1,0:T(2,128)}), f32[16,2,128]{2,1,0:T(2,128)S(1)}, u32[]{:S(2)}, u32[]{:S(2)}) async-start(f32[16,2,128]{2,1,0:T(2,128)} %bitcast.34), calls=%async_computation.5 | async-start | bytes 32768 | tf_op jit(solution)/shard_map/all_to_all | solution.py:97
  342.9 11.0 %all-to-all-start.6 = ((f32[16,2,128]{2,1,0:T(2,128)}), f32[16,2,128]{2,1,0:T(2,128)S(1)}, u32[]{:S(2)}, u32[]{:S(2)}) async-start(f32[16,2,128]{2,1,0:T(2,128)} %copy.27), calls=%async_computation.6 | async-start | bytes 32768 | tf_op jit(solution)/shard_map/all_to_all | solution.py:94
  355.2 11.2 %all-to-all-start.7 = ((f32[16,2,128]{2,1,0:T(2,128)}), f32[16,2,128]{2,1,0:T(2,128)S(1)}, u32[]{:S(2)}, u32[]{:S(2)}) async-start(f32[16,2,128]{2,1,0:T(2,128)} %bitcast.46), calls=%async_computation.7 | async-start | bytes 32768 | tf_op jit(solution)/shard_map/all_to_all | solution.py:97
  373.7 4.9 copy-start
  378.6 16.6 %copy-start.2 = (bf16[8,8,256,128]{2,3,1,0:T(8,128)(2,1)}, bf16[8,8,256,128]{2,3,1,0:T(8,128)(2,1)S(1)}, u32[]{:S(2)}) copy-start(bf16[8,8,256,128]{2,3,1,0:T(8,128)(2,1)S(1)} %get-tuple-element.11) | copy-start | bytes 12582916
  398.8 92.4 %all-to-all-start.9 = ((f32[16,2,128]{2,1,0:T(2,128)}), f32[16,2,128]{2,1,0:T(2,128)S(1)}, u32[]{:S(2)}, u32[]{:S(2)}) async-start(f32[16,2,128]{2,1,0:T(2,128)} %copy.28), calls=%async_computation.9 | async-start | bytes 32768 | tf_op jit(solution)/shard_map/all_to_all | solution.py:126
  491.2 240.8 %all-to-all-start.8 = ((f32[16,2,128,1024]{3,2,1,0:T(8,128)}), f32[16,2,128,1024]{3,2,1,0:T(8,128)}, u32[]{:S(2)}, u32[]{:S(2)}) async-start(f32[16,2,128,1024]{3,2,1,0:T(8,128)} %bitcast.176), calls=%async_computation.8 | async-start | bytes 33554432 | tf_op jit(solution)/shard_map/all_to_all | solution.py:119
where the time goes:
time: 768 us; the launch traced here: 762 us
  waiting for transfers between devices  373 us (49%)
  matrix products  103 us (13%)
  other arithmetic  94.8 us (12%)
  blocking collectives  88.8 us (12%)
  local copies, waits for them, and re-layouts  57.9 us (8%)
  starting transfers between devices  42 us (5%)
    all_to_all x1, waiting for transfers between devices, body(): lax.all_to_all(gathered_sums.reshape(rows_count, use_count, CB, D), 'rows...  233 us
    all_to_all x1, waiting for transfers between devices, body(): lax.all_to_all(lists_norm[local_in], 'rows', split_axis=0, concat_axis=0,...  116 us
    scatter-add x8, other arithmetic, body(): gathered_sums = gathered_sums.at[slot_target[:, slot_number]].add(slot_part)  75.8 us
    psum x1, blocking collectives, body(): weight_sum = lax.psum(jnp.sum(row_weight), ('rows', 'cents'))  65.5 us
    dot_general x4, matrix products, body(): row_sums = jnp.einsum('bkrc,bkc->br', kernel, picked, precision=HIGHEST)  27.9 us
    dot_general x3, matrix products, body(): jnp.einsum('bkrc,br->bkc', kernel, row_scale, precision=HIGHEST)  26 us
    dot_general x8, matrix products, body(): jnp.einsum('brc,brd->bcd', transport_half[:, slot_number], rows_norm, pre...  24.3 us
    unnamed x17, local copies, waits for them, and re-layouts  15.5 us
  transfers between devices with their start and end apart: 8, of which 6 were waited for; matrix products, arithmetic and copies ran while one was open for 14% of the time, Pallas kernels for 0%

commit v1 on v0

v1 whole, which is shorter than its diff:
```python
import jax
import jax.numpy as jnp
from jax import lax
from jax.experimental import pallas as pl
from jax.experimental.pallas import tpu as pltpu
from jax.sharding import PartitionSpec as P

D = 1024
RB = 256
CB = 128
MAXC = 8
USE = 2
ITERS = 3
NBD = 8
CBD = 16
NR = 16
NC = 8
ND = NR * USE
NDX = ND + 8
K_TOTAL = NR * NC * CBD * CB
ROWS_X = USE * CB * (D // 128)
ROWS_P = ROWS_X + 16

BETA = 32.0
EPSILON = 1e-06
PRIOR = 0.25
F32 = jnp.float32
BF16 = jnp.bfloat16


def unit_rows(values):
    widened = values.astype(F32)
    mean = jnp.sum(widened * widened, axis=-1, keepdims=True) * (1.0 / D)
    return (widened * lax.rsqrt(mean + EPSILON)).astype(BF16)


def rows_kernel(groups_ref, out_ref):
    out_ref[...] = unit_rows(groups_ref[...])


def normalize_rows(groups):
    step = 512
    return pl.pallas_call(
        rows_kernel,
        grid=(groups.shape[0] // step,),
        in_specs=[pl.BlockSpec((step, D), lambda i: (i, 0))],
        out_specs=pl.BlockSpec((step, D), lambda i: (i, 0)),
        out_shape=jax.ShapeDtypeStruct(groups.shape, BF16),
        name="rows_norm",
    )(groups)


def pick_kernel(wanted_ref, *refs):
    out_ref = refs[-1]
    for n, block in enumerate(refs[:-1]):
        out_ref[n] = unit_rows(block[0])


def pick_lists(centroids, wanted):
    per = 4
    specs = [
        pl.BlockSpec((1, CB, D), lambda i, w, n=n: (w[i * per + n], 0, 0)) for n in range(per)
    ]
    return pl.pallas_call(
        pick_kernel,
        grid_spec=pltpu.PrefetchScalarGridSpec(
            num_scalar_prefetch=1,
            grid=(ND // per,),
            in_specs=specs,
            out_specs=pl.BlockSpec((per, CB, D), lambda i, w: (i, 0, 0)),
        ),
        out_shape=jax.ShapeDtypeStruct((ND, CB, D), BF16),
        name="pick_lists",
    )(wanted, *([centroids] * per))


def column_pass(kernel_ref, row_scale, dist_ref, b, parts_ref):
    for k in range(MAXC):
        part = jnp.sum(kernel_ref[0, k] * row_scale, axis=0, keepdims=True)
        d = dist_ref[b * MAXC + k]
        parts_ref[pl.ds(d, 1), :] += part


def spread(parts_ref, mass, out_ref):
    parts = parts_ref[...]
    for r in range(NR):
        out_ref[r, :ND, :] = parts
        out_ref[r, ND:, :] = mass


def scores_kernel(dist_ref, count_ref, *refs):
    rows_ref, weight_ref, mass_ref = refs[:3]
    lists = refs[3 : 3 + MAXC]
    kernel_ref, out_ref, parts_ref = refs[3 + MAXC :]
    b = pl.program_id(0)
    count = count_ref[b]
    rows = rows_ref[0]

    @pl.when(b == 0)
    def _():
        parts_ref[...] = jnp.zeros_like(parts_ref)

    total = jnp.zeros((RB, CB), F32)
    for k in range(0, MAXC, 2):
        pair = jnp.concatenate([lists[k][0], lists[k + 1][0]], axis=0)
        scores = lax.dot_general(
            rows, pair, (((1,), (1,)), ((), ())), preferred_element_type=F32
        )
        grown = jnp.exp(scores * (BETA / D))
        for n in range(2):
            live = jnp.where(k + n < count, grown[:, n * CB : (n + 1) * CB], 0.0)
            kernel_ref[0, k + n] = live
            total = total + live
    row_scale = weight_ref[0] / jnp.sum(total, axis=1, keepdims=True)
    column_pass(kernel_ref, row_scale, dist_ref, b, parts_ref)

    @pl.when(b == NBD - 1)
    def _():
        spread(parts_ref, mass_ref[...], out_ref)


def first_pass(dist, counts, rows, weights, mass, lists):
    fixed = lambda *shape: pl.BlockSpec(shape, lambda b, d, c: (0,) * len(shape))
    list_specs = [
        pl.BlockSpec((1, CB, D), lambda b, d, c, k=k: (d[b * MAXC + k], 0, 0)) for k in range(MAXC)
    ]
    return pl.pallas_call(
        scores_kernel,
        grid_spec=pltpu.PrefetchScalarGridSpec(
            num_scalar_prefetch=2,
            grid=(NBD,),
            in_specs=[
                pl.BlockSpec((1, RB, D), lambda b, d, c: (b, 0, 0)),
                pl.BlockSpec((1, RB, CB), lambda b, d, c: (b, 0, 0)),
                fixed(8, CB),
            ]
            + list_specs,
            out_specs=[
                pl.BlockSpec((1, MAXC, RB, CB), lambda b, d, c: (b, 0, 0, 0)),
                fixed(NR, NDX, CB),
            ],
            scratch_shapes=[pltpu.VMEM((ND, CB), F32)],
        ),
        out_shape=[
            jax.ShapeDtypeStruct((NBD, MAXC, RB, CB), F32),
            jax.ShapeDtypeStruct((NR, NDX, CB), F32),
        ],
        name="scores",
    )(dist, counts, rows, weights, mass, *([lists] * MAXC))


def new_scales(got_ref, same_ref, scales_ref):
    straight = jnp.zeros((ND, CB), F32)
    crossed = jnp.zeros((ND, CB), F32)
    mass = jnp.zeros((8, CB), F32)
    for r in range(NR):
        got = got_ref[r, :ND, :]
        straight = straight + same_ref[0, r] * got
        crossed = crossed + same_ref[1, r] * got
        mass = mass + got_ref[r, ND:, :]
    even = lax.broadcasted_iota(jnp.int32, (ND, CB), 0) % 2 == 0
    swapped = jnp.where(even, jnp.roll(crossed, -1, axis=0), jnp.roll(crossed, 1, axis=0))
    target = mass * (1.0 / K_TOTAL)
    column = straight + swapped
    scales_ref[...] = target[:1] / (column + PRIOR * target[:1])
    return target


def row_pass(kernel_ref, weight_ref, scales_ref, dist_ref, b):
    total = jnp.zeros((RB, CB), F32)
    for k in range(MAXC):
        d = dist_ref[b * MAXC + k]
        total = total + kernel_ref[0, k] * scales_ref[pl.ds(d, 1), :]
    return weight_ref[0] / jnp.sum(total, axis=1, keepdims=True)


def turn(dist, kernel, weights, got, same, mass):
    fixed = lambda *shape: pl.BlockSpec(shape, lambda b, d: (0,) * len(shape))

    def body(dist_ref, kernel_ref, weight_ref, got_ref, same_ref, mass_ref, out_ref, scales_ref, parts_ref):
        b = pl.program_id(0)

        @pl.when(b == 0)
        def _():
            new_scales(got_ref, same_ref, scales_ref)
            parts_ref[...] = jnp.zeros_like(parts_ref)

        row_scale = row_pass(kernel_ref, weight_ref, scales_ref, dist_ref, b)
        column_pass(kernel_ref, row_scale, dist_ref, b, parts_ref)

        @pl.when(b == NBD - 1)
        def _():
            spread(parts_ref, mass_ref[...], out_ref)

    return pl.pallas_call(
        body,
        grid_spec=pltpu.PrefetchScalarGridSpec(
            num_scalar_prefetch=1,
            grid=(NBD,),
            in_specs=[
                pl.BlockSpec((1, MAXC, RB, CB), lambda b, d: (b, 0, 0, 0)),
                pl.BlockSpec((1, RB, CB), lambda b, d: (b, 0, 0)),
                fixed(NR, NDX, CB),
                fixed(2, NR, ND, CB),
                fixed(8, CB),
            ],
            out_specs=fixed(NR, NDX, CB),
            scratch_shapes=[pltpu.VMEM((ND, CB), F32), pltpu.VMEM((ND, CB), F32)],
        ),
        out_shape=jax.ShapeDtypeStruct((NR, NDX, CB), F32),
        name="turn",
    )(dist, kernel, weights, got, same, mass)


def final_kernel(
    dist_ref,
    kernel_ref,
    weight_ref,
    rows_ref,
    got_ref,
    same_ref,
    out_ref,
    target_ref,
    scales_ref,
    parts_ref,
    rows_keep,
    plan_keep,
    order_ref,
    seen_ref,
):
    step = pl.program_id(0)

    @pl.when(step == 0)
    def _():
        target_ref[...] = new_scales(got_ref, same_ref, scales_ref)
        parts_ref[...] = jnp.zeros_like(parts_ref)

        @pl.loop(0, ND)
        def _(d):
            seen_ref[d] = 0

        @pl.loop(0, NBD * MAXC)
        def _(p):
            d = dist_ref[p]
            n = seen_ref[d]
            seen_ref[d] = n + 1
            holder = d // 2
            order_ref[holder * 4 + jnp.where(d % 2 == 0, n, 3 - n)] = p

    @pl.when(step < NBD)
    def _():
        b = step
        row_scale = row_pass(kernel_ref, weight_ref, scales_ref, dist_ref, b)
        for k in range(MAXC):
            d = dist_ref[b * MAXC + k]
            plan = row_scale * kernel_ref[0, k] * scales_ref[pl.ds(d, 1), :]
            parts_ref[pl.ds(d, 1), :] += jnp.sum(plan, axis=0, keepdims=True)
            plan_keep[b * MAXC + k] = jnp.transpose(plan).astype(BF16)
        rows_keep[b] = rows_ref[0]

    @pl.when(step >= NBD)
    def _():
        holder = step - NBD
        slots = [order_ref[holder * 4 + n] for n in range(4)]
        plans = [plan_keep[p] for p in slots]
        first = seen_ref[holder * 2]

        def emit(u, chosen):
            left = jnp.concatenate([plans[n] for n in chosen], axis=1)
            right = jnp.concatenate([rows_keep[slots[n] // MAXC] for n in chosen], axis=0)
            total = jnp.dot(left, right, preferred_element_type=F32)
            for c in range(D // 128):
                at = c * USE * CB + u * CB
                out_ref[0, at : at + CB, :] = total[:, c * 128 : (c + 1) * 128].astype(BF16)

        for split in (1, 2, 3):

            @pl.when(first == split)
            def _(split=split):
                emit(0, range(split))
                emit(1, range(split, 4))

        rest = parts_ref[pl.ds(holder * 2, 2), :]
        terms = []
        for _ in range(3):
            piece = rest.astype(BF16).astype(F32)
            terms.append(piece)
            rest = rest - piece
        terms.append(jnp.zeros((10, CB), F32))
        out_ref[0, ROWS_X:, :] = jnp.concatenate(terms, axis=0).astype(BF16)


def final_pass(dist, kernel, weights, rows, got, same):
    fixed = lambda *shape: pl.BlockSpec(shape, lambda s, d: (0,) * len(shape))
    early = lambda s: jnp.minimum(s, NBD - 1)
    return pl.pallas_call(
        final_kernel,
        grid_spec=pltpu.PrefetchScalarGridSpec(
            num_scalar_prefetch=1,
            grid=(NBD + NR,),
            in_specs=[
                pl.BlockSpec((1, MAXC, RB, CB), lambda s, d: (early(s), 0, 0, 0)),
                pl.BlockSpec((1, RB, CB), lambda s, d: (early(s), 0, 0)),
                pl.BlockSpec((1, RB, D), lambda s, d: (early(s), 0, 0)),
                fixed(NR, NDX, CB),
                fixed(2, NR, ND, CB),
            ],
            out_specs=[
                pl.BlockSpec((1, ROWS_P, 128), lambda s, d: (jnp.maximum(s - NBD, 0), 0, 0)),
                fixed(8, CB),
            ],
            scratch_shapes=[
                pltpu.VMEM((ND, CB), F32),
                pltpu.VMEM((ND, CB), F32),
                pltpu.VMEM((NBD, RB, D), BF16),
                pltpu.VMEM((NBD * MAXC, CB, RB), BF16),
                pltpu.SMEM((NBD * MAXC,), jnp.int32),
                pltpu.SMEM((ND,), jnp.int32),
            ],
        ),
        out_shape=[
            jax.ShapeDtypeStruct((NR, ROWS_P, 128), BF16),
            jax.ShapeDtypeStruct((8, CB), F32),
        ],
        name="final_pass",
    )(dist, kernel, weights, rows, got, same)


def merge_kernel(wanted_ref, got_ref, extra_ref, target_ref, out_ref, load_ref, order_ref, start_ref):
    step = pl.program_id(0)

    @pl.when(step == 0)
    def _():
        @pl.loop(0, CBD + 1)
        def _(j):
            start_ref[j] = 0

        @pl.loop(0, ND)
        def _(i):
            j = wanted_ref[i]
            start_ref[j + 1] = start_ref[j + 1] + 1

        @pl.loop(0, CBD)
        def _(j):
            start_ref[j + 1] = start_ref[j + 1] + start_ref[j]

        @pl.loop(0, ND)
        def _(n):
            i = ND - 1 - n
            j = wanted_ref[i]
            at = start_ref[j + 1] - 1
            start_ref[j + 1] = at
            order_ref[at] = i

        load_ref[...] = jnp.zeros_like(load_ref)
        for r in range(NR):
            terms = extra_ref[r].astype(F32)
            for u in range(USE):
                mass = terms[u : u + 1] + terms[u + 2 : u + 3] + terms[u + 4 : u + 5]
                load_ref[pl.ds(wanted_ref[r * USE + u], 1), :] += mass
        load_ref[...] = load_ref[...] / target_ref[:1]

    for j in range(CBD):
        begin = start_ref[j + 1]
        end = start_ref[j + 2] if j + 1 < CBD else ND

        def add(n, total):
            i = order_ref[n]
            at = pl.multiple_of((i % USE) * CB, CB)
            return total + got_ref[i // USE, pl.ds(at, CB), :].astype(F32)

        out_ref[j] = lax.fori_loop(begin, end, add, jnp.zeros((CB, 128), F32))


def merge(wanted, got, target):
    return pl.pallas_call(
        merge_kernel,
        grid_spec=pltpu.PrefetchScalarGridSpec(
            num_scalar_prefetch=1,
            grid=(D // 128,),
            in_specs=[
                pl.BlockSpec((NR, USE * CB, 128), lambda s, w: (0, s, 0)),
                pl.BlockSpec((NR, 16, 128), lambda s, w: (0, ROWS_X // 16, 0)),
                pl.BlockSpec((8, CB), lambda s, w: (0, 0)),
            ],
            out_specs=[
                pl.BlockSpec((CBD, CB, 128), lambda s, w: (0, 0, s)),
                pl.BlockSpec((CBD, CB), lambda s, w: (0, 0)),
            ],
            scratch_shapes=[pltpu.SMEM((ND,), jnp.int32), pltpu.SMEM((CBD + 2,), jnp.int32)],
        ),
        out_shape=[
            jax.ShapeDtypeStruct((CBD, CB, D), F32),
            jax.ShapeDtypeStruct((CBD, CB), F32),
        ],
        name="merge",
    )(wanted, got, got, target)


def exchange(values):
    return lax.all_to_all(values, "rows", split_axis=0, concat_axis=0, tiled=True)


def body(groups, centroids, row_weight, block_ids, block_counts):
    flat = block_ids.reshape(-1)
    holder = flat // (CBD * NC)
    local = flat % CBD
    of_holder = jnp.arange(NR, dtype=jnp.int32)[:, None] == holder[None, :]
    low = jnp.min(jnp.where(of_holder, local[None, :], CBD), axis=1)
    high = jnp.max(jnp.where(of_holder, local[None, :], -1), axis=1)
    table = jnp.stack([low, high], axis=1).reshape(1, 1, ND)
    tables = exchange(jnp.broadcast_to(table, (NR, 1, ND))).reshape(NR, ND)
    me = lax.axis_index("rows")
    wanted = lax.dynamic_slice(tables, (0, me * USE), (NR, USE)).reshape(-1)

    low_here = jnp.sum(jnp.where(of_holder, low[:, None], 0), axis=0)
    dist = holder * USE + (local != low_here).astype(jnp.int32)

    mass = jnp.broadcast_to(jnp.sum(row_weight), (8, CB))
    for bit in (1, 2, 4):
        mass = mass + lax.ppermute(mass, "cents", [(i, i ^ bit) for i in range(NC)])

    mine = table.reshape(ND)
    other = jnp.stack([high, low], axis=1).reshape(ND)
    same = jnp.stack([tables == mine[None, :], tables == other[None, :]]).astype(F32)
    same = jnp.broadcast_to(same[..., None], (2, NR, ND, CB))
    weights = jnp.broadcast_to(row_weight.reshape(NBD, RB, 1), (NBD, RB, CB))

    rows = normalize_rows(groups).reshape(NBD, RB, D)
    picked = pick_lists(centroids.reshape(CBD, CB, D), wanted).reshape(NR, USE * CB, D)
    picked, rows, weights, same, mass, dist = lax.optimization_barrier(
        (picked, rows, weights, same, mass, dist)
    )
    lists = exchange(picked).reshape(ND, CB, D)

    kernel, parts = first_pass(dist, block_counts, rows, weights, mass, lists)
    got = exchange(parts)
    for _ in range(ITERS - 1):
        got = exchange(turn(dist, kernel, weights, got, same, mass))
    sums, target = final_pass(dist, kernel, weights, rows, got, same)
    totals, load = merge(wanted, exchange(sums), target)
    return totals.reshape(-1, D), load.reshape(-1)


def solution(mesh):
    placed = (
        P(("rows", "cents"), None),
        P(("rows", "cents"), None),
        P(("rows", "cents")),
        P(("rows", "cents"), None),
        P(("rows", "cents")),
    )
    return jax.shard_map(
        body,
        mesh=mesh,
        in_specs=placed,
        out_specs=(P(("rows", "cents"), None), P(("rows", "cents"))),
        check_vma=False,
    )
```

time: 768 us -> 348 us (0.45)
  waiting for transfers between devices: 373 us -> 2.03 us
  blocking collectives: 88.8 us -> 240 us
  matrix products: 103 us -> 0 us
  other arithmetic: 94.8 us -> 3.98 us
  Pallas kernels: 0 us -> 80.5 us
  local copies, waits for them, and re-layouts: 57.9 us -> 6.08 us
  starting transfers between devices: 42 us -> 13 us
    all_to_all x8 -> x1, waiting for transfers between devices: 373 us -> 0.01 us  [exchange(): lax.all_to_all(values, 'rows', split_axis=0, concat_axis=0, tiled=True)]
    all_to_all x2 -> x5, blocking collectives: 23.3 us -> 240 us  [exchange(): lax.all_to_all(values, 'rows', split_axis=0, concat_axis=0, tiled=True)]
    dot_general x25 -> x0, matrix products: 103 us -> none  [the longest x4 27.9 us: body(): row_sums = jnp.einsum('bkrc,bkc->br', kernel, picked, precision=HIGHEST)]
    pallas_call x0 -> x7, Pallas kernels: none -> 80.5 us  [the longest x1 21.4 us: final_pass(): pl.pallas_call(final_kernel, grid_spec=pltpu.PrefetchScalarGridSpec(num_s...]
    scatter-add x8 -> x0, other arithmetic: 75.8 us -> none  [body(): gathered_sums = gathered_sums.at[slot_target[:, slot_number]].add(slot_part)]
    psum x1 -> x0, blocking collectives: 65.5 us -> none  [body(): weight_sum = lax.psum(jnp.sum(row_weight), ('rows', 'cents'))]
    all_to_all x8 -> x1, starting transfers between devices: 42 us -> 7.99 us  [exchange(): lax.all_to_all(values, 'rows', split_axis=0, concat_axis=0, tiled=True)]
    gather x10 -> x0, local copies, waits for them, and re-layouts: 23.9 us -> none  [the longest x1 11 us: body(): arrived.reshape(-1, CB, D)[distinct_of_pair]]
  transfers between devices with their start and end apart: 8 -> 4, of which waited for: 6 -> 1; matrix products, arithmetic and copies ran while one was open for 14% -> 1% of each run, Pallas kernels for 0% -> 4%
where the time goes in v1:
time: 348 us; the launch traced here: 346 us
  blocking collectives  240 us (69%)
  Pallas kernels  80.5 us (23%)
  starting transfers between devices  13 us (4%)
  local copies, waits for them, and re-layouts  6.08 us (2%)
  other arithmetic  3.98 us (1%)
    all_to_all x5, blocking collectives, exchange(): lax.all_to_all(values, 'rows', split_axis=0, concat_axis=0, tiled=True)  240 us
    pallas_call x1, Pallas kernels, final_pass(): pl.pallas_call(final_kernel, grid_spec=pltpu.PrefetchScalarGridSpec(num_s...  21.4 us
    pallas_call x2, Pallas kernels, turn(): pl.pallas_call(body, grid_spec=pltpu.PrefetchScalarGridSpec(num_scalar_pr...  16.2 us
    pallas_call x1, Pallas kernels, first_pass(): pl.pallas_call(scores_kernel, grid_spec=pltpu.PrefetchScalarGridSpec(num_...  15.7 us
    pallas_call x1, Pallas kernels, merge(): pl.pallas_call(merge_kernel, grid_spec=pltpu.PrefetchScalarGridSpec(num_s...  11.7 us
    pallas_call x1, Pallas kernels, pick_lists(): pl.pallas_call(pick_kernel, grid_spec=pltpu.PrefetchScalarGridSpec(num_sc...  10.2 us
    all_to_all x1, starting transfers between devices, exchange(): lax.all_to_all(values, 'rows', split_axis=0, concat_axis=0, tiled=True)  7.99 us
  transfers between devices with their start and end apart: 4, of which 1 were waited for; matrix products, arithmetic and copies ran while one was open for 1% of the time, Pallas kernels for 4%

profile of v1, /device:TPU:0, one launch (start us, length us, event | category | flops | bytes accessed | tf_op | source)
XLA Modules:
  0.0 345.8 jit_solution(14617885529072108954)
XLA Ops:
  0.6 0.8 reshape.188
  2.3 8.0 %all-to-all-start = ((s32[16,1,32]{2,1,0:T(1,128)}), s32[16,1,32]{2,1,0:T(1,128)S(1)}, u32[]{:S(2)}, u32[]{:S(2)}) async-start(s32[16,1,32]{2,1,0:T(1,128)} %broadcast_in_dim.62), calls=%async_computation | async-start | bytes 16384 | tf_op jit(solution)/shard_map/all_to_all | solution.py:401
  10.3 1.3 reduce_sum.18
  11.6 0.6 broadcast_in_dim.66
  13.0 0.7 broadcast_in_dim.63
  13.9 5.2 %rows_norm.1 = bf16[2048,1024]{1,0:T(8,128)(2,1)} custom-call(bf16[2048,1024]{1,0:T(8,128)(2,1)} %groups_ref.1), custom_call_target="tpu_custom_call" | custom-call | tf_op jit(solution)/shard_map/rows_norm/pallas_call | solution.py:43
  19.1 0.6 broadcast_add_fusion
  19.8 1.7 collective-permute-start.1
  21.4 2.0 collective-permute-done.1
  23.5 0.6 fusion.1
  24.1 3.3 collective-permute-start.2
  28.1 10.2 %pick_lists.1 = bf16[32,128,1024]{2,1,0:T(8,128)(2,1)} custom-call(s32[32]{0:T(128)} %reshape.189.wanted_ref, bf16[16,128,1024]{2,1,0:T(8,128)(2,1)} %bitcast.20, bf16[16,128,1024]{2,1,0:T(8,128)(2,1)} %bitcast.21, bf16[16,128,1024]{2,1,0:T(8,128)(2,1)} %bitcast.22, bf16[16,128,1024]{2,1,0:T(8,128)(2,1)} %bitcast.23), custom_call_target="tpu_custom_call" | custom-call | tf_op jit(solution)/shard_map/pick_lists/pallas_call | solution.py:64
  38.9 1.0 broadcast_in_dim.65.same_ref
  39.8 1.4 broadcast_in_dim.64.refs_1_.weight_ref
  41.2 102.6 %all_to_all.30 = bf16[16,256,1024]{2,1,0:T(8,128)(2,1)} all-to-all(bf16[16,256,1024]{2,1,0:T(8,128)(2,1)} %bitcast.26), channel_id=1, replica_groups=mesh['rows'=16,'cents'=8] {'rows'}, dimensions={0} | all-to-all | bytes 16777216 | tf_op jit(solution)/shard_map/all_to_all | solution.py:401
  143.8 15.7 %scores.1 = (f32[8,8,256,128]{3,2,1,0:T(8,128)}, f32[16,40,128]{2,1,0:T(8,128)}) custom-call(s32[64]{0:T(128)} %fusion.dist_ref, s32[8]{0:T(128)} %count_ref.1, bf16[8,256,1024]{2,1,0:T(8,128)(2,1)} %bitcast.24, f32[8,256,128]{2,1,0:T(8,128)} %broadcast_in_dim.64.refs_1_.weight_ref, f32[8,128]{1,0:T(8,128)} %add.34.refs_2_.mass_ref, ...), custom_call_target="tpu_custom_call" | custom-call | tf_op jit(solution)/shard_map/scores/pallas_call | solution.py:127
  159.6 13.2 %all_to_all.31.got_ref = f32[16,40,128]{2,1,0:T(8,128)} all-to-all(f32[16,40,128]{2,1,0:T(8,128)} %get-tuple-element.20), channel_id=1, replica_groups=mesh['rows'=16,'cents'=8] {'rows'}, dimensions={0} | all-to-all | bytes 655360 | tf_op jit(solution)/shard_map/all_to_all | solution.py:401
  172.8 8.1 %turn.2 = f32[16,40,128]{2,1,0:T(8,128)} custom-call(s32[64]{0:T(128)} %fusion.dist_ref, f32[8,8,256,128]{3,2,1,0:T(8,128)} %get-tuple-element.19.kernel_ref, f32[8,256,128]{2,1,0:T(8,128)} %broadcast_in_dim.64.refs_1_.weight_ref, f32[16,40,128]{2,1,0:T(8,128)} %all_to_all.31.got_ref, f32[2,16,32,128]{3,2,1,0:T(8,128)} %broadcast_in_dim.65.same_ref, ...), custom_call_target="tpu_custom_call" | custom-call | tf_op jit(solution)/shard_map/turn/pallas_call | solution.py:195
  180.9 13.2 %all_to_all.32.got_ref = f32[16,40,128]{2,1,0:T(8,128)} all-to-all(f32[16,40,128]{2,1,0:T(8,128)} %turn.2), channel_id=1, replica_groups=mesh['rows'=16,'cents'=8] {'rows'}, dimensions={0} | all-to-all | bytes 655360 | tf_op jit(solution)/shard_map/all_to_all | solution.py:401
  194.1 8.1 %turn.3 = f32[16,40,128]{2,1,0:T(8,128)} custom-call(s32[64]{0:T(128)} %fusion.dist_ref, f32[8,8,256,128]{3,2,1,0:T(8,128)} %get-tuple-element.19.kernel_ref, f32[8,256,128]{2,1,0:T(8,128)} %broadcast_in_dim.64.refs_1_.weight_ref, f32[16,40,128]{2,1,0:T(8,128)} %all_to_all.32.got_ref, f32[2,16,32,128]{3,2,1,0:T(8,128)} %broadcast_in_dim.65.same_ref, ...), custom_call_target="tpu_custom_call" | custom-call | tf_op jit(solution)/shard_map/turn/pallas_call | solution.py:195
  202.2 13.2 %all_to_all.33.got_ref = f32[16,40,128]{2,1,0:T(8,128)} all-to-all(f32[16,40,128]{2,1,0:T(8,128)} %turn.3), channel_id=1, replica_groups=mesh['rows'=16,'cents'=8] {'rows'}, dimensions={0} | all-to-all | bytes 655360 | tf_op jit(solution)/shard_map/all_to_all | solution.py:401
  215.5 21.4 %final_pass.1 = (bf16[16,2064,128]{2,1,0:T(8,128)(2,1)}, f32[8,128]{1,0:T(8,128)}) custom-call(s32[64]{0:T(128)} %fusion.dist_ref, f32[8,8,256,128]{3,2,1,0:T(8,128)} %get-tuple-element.19.kernel_ref, f32[8,256,128]{2,1,0:T(8,128)} %broadcast_in_dim.64.refs_1_.weight_ref, bf16[8,256,1024]{2,1,0:T(8,128)(2,1)} %bitcast.25, ...), custom_call_target="tpu_custom_call" | custom-call | tf_op jit(solution)/shard_map/final_pass/pallas_call | solution.py:296
  236.9 97.3 %all_to_all.34.got_ref.extra_ref = bf16[16,2064,128]{2,1,0:T(8,128)(2,1)} all-to-all(bf16[16,2064,128]{2,1,0:T(8,128)(2,1)} %get-tuple-element.22), channel_id=1, replica_groups=mesh['rows'=16,'cents'=8] {'rows'}, dimensions={0} | all-to-all | bytes 16908288 | tf_op jit(solution)/shard_map/all_to_all | solution.py:401
  334.1 11.7 %merge.1 = (f32[16,128,1024]{2,1,0:T(8,128)}, f32[16,128]{1,0:T(8,128)}) custom-call(s32[32]{0:T(128)} %reshape.189.wanted_ref, bf16[16,2064,128]{2,1,0:T(8,128)(2,1)} %all_to_all.34.got_ref.extra_ref, bf16[16,2064,128]{2,1,0:T(8,128)(2,1)} %all_to_all.34.got_ref.extra_ref, f32[8,128]{1,0:T(8,128)} %get-tuple-element.23.target_ref), custom_call_target="tpu_custom_call" | custom-call | tf_op jit(solution)/shard_map/merge/pallas_call | solution.py:376
  (19 shorter events, 3.1 us)
Async XLA Ops:
  2.3 19.1 %all-to-all-start = ((s32[16,1,32]{2,1,0:T(1,128)}), s32[16,1,32]{2,1,0:T(1,128)S(1)}, u32[]{:S(2)}, u32[]{:S(2)}) async-start(s32[16,1,32]{2,1,0:T(1,128)} %broadcast_in_dim.62), calls=%async_computation | async-start | bytes 16384 | tf_op jit(solution)/shard_map/all_to_all | solution.py:401
  12.3 6.8 %collective-permute-start = (f32[8,128]{1,0:T(8,128)S(1)}, f32[8,128]{1,0:T(8,128)S(1)}, u32[]{:S(2)}, u32[]{:S(2)}) collective-permute-start(f32[8,128]{1,0:T(8,128)S(1)} %broadcast_in_dim.66), channel_id=1, source_target_pairs={{0,1},{1,0},{2,3},{3,2},{4,5},{5,4},{6,7},{7,6},{8,9},{9,8},{10,11... | collective-permute-start | bytes 12296 | tf_op jit(solution)/shard_map/ppermute | solution.py:421
  19.8 3.7 %collective-permute-start.1 = (f32[8,128]{1,0:T(8,128)S(1)}, f32[8,128]{1,0:T(8,128)S(1)}, u32[]{:S(2)}, u32[]{:S(2)}) collective-permute-start(f32[8,128]{1,0:T(8,128)S(1)} %broadcast_add_fusion), channel_id=1, source_target_pairs={{0,2},{1,3},{2,0},{3,1},{4,6},{5,7},{6,4},{7,5},{8,10},{9,11},{10,... | collective-permute-start | bytes 12296 | tf_op jit(solution)/shard_map/ppermute | solution.py:421
  24.1 14.2 %collective-permute-start.2 = (f32[8,128]{1,0:T(8,128)S(1)}, f32[8,128]{1,0:T(8,128)S(1)}, u32[]{:S(2)}, u32[]{:S(2)}) collective-permute-start(f32[8,128]{1,0:T(8,128)S(1)} %fusion.1), channel_id=1, source_target_pairs={{0,4},{1,5},{2,6},{3,7},{4,0},{5,1},{6,2},{7,3},{8,12},{9,13},{10,... | collective-permute-start | bytes 12296 | tf_op jit(solution)/shard_map/ppermute | solution.py:421

commit v2 on v1

v2 whole, which is shorter than its diff:
```python
import jax
import jax.numpy as jnp
from jax import lax
from jax.experimental import pallas as pl
from jax.experimental.pallas import tpu as pltpu
from jax.sharding import PartitionSpec as P

D = 1024
RB = 256
CB = 128
MAXC = 8
USE = 2
ITERS = 3
NBD = 8
CBD = 16
NR = 16
NC = 8
ND = NR * USE
DEVICES = NR * NC
K_TOTAL = DEVICES * CBD * CB
ROWS_X = USE * CB * (D // 128)
ROWS_P = ROWS_X + 16

BETA = 32.0
EPSILON = 1e-06
PRIOR = 0.25
F32 = jnp.float32
BF16 = jnp.bfloat16
HELD = pl.BlockSpec(memory_space=pltpu.VMEM)
LIMIT = pltpu.CompilerParams(vmem_limit_bytes=40 << 20)


def unit_rows(values):
    widened = values.astype(F32)
    mean = jnp.sum(widened * widened, axis=-1, keepdims=True) * (1.0 / D)
    return (widened * lax.rsqrt(mean + EPSILON)).astype(BF16)


def table_kernel(ids_ref, weight_ref, table_ref, dist_ref, low_ref, high_ref):
    @pl.loop(0, NR)
    def _(o):
        low_ref[o] = CBD
        high_ref[o] = -1

    @pl.loop(0, NBD)
    def _(b):
        for k in range(MAXC):
            number = ids_ref[b, k]
            holder = number // (CBD * NC)
            local = number % CBD
            low_ref[holder] = jnp.minimum(low_ref[holder], local)
            high_ref[holder] = jnp.maximum(high_ref[holder], local)

    @pl.loop(0, NBD)
    def _(b):
        for k in range(MAXC):
            number = ids_ref[b, k]
            holder = number // (CBD * NC)
            local = number % CBD
            dist_ref[b * MAXC + k] = holder * USE + jnp.where(local != low_ref[holder], 1, 0)

    weight = jnp.sum(jnp.sum(weight_ref[...], axis=0, keepdims=True), axis=1, keepdims=True)
    lane = lax.broadcasted_iota(jnp.int32, (1, CB), 1)
    numbers = jnp.zeros((1, CB), jnp.int32)
    for o in range(NR):
        low = low_ref[o]
        high = high_ref[o]
        is_low = (lane == USE * o) | (lane == ND + USE * o + 1)
        is_high = (lane == USE * o + 1) | (lane == ND + USE * o)
        numbers = jnp.where(is_low, low, jnp.where(is_high, high, numbers))
    row = jnp.where(lane < 2 * ND, numbers.astype(F32), jnp.broadcast_to(weight, (1, CB)))
    table_ref[...] = jnp.broadcast_to(row, (DEVICES, CB))


def make_table(block_ids, weight_rows):
    return pl.pallas_call(
        table_kernel,
        in_specs=[pl.BlockSpec(memory_space=pltpu.SMEM), HELD],
        out_specs=[HELD, pl.BlockSpec(memory_space=pltpu.SMEM)],
        out_shape=[
            jax.ShapeDtypeStruct((DEVICES, CB), F32),
            jax.ShapeDtypeStruct((NBD * MAXC,), jnp.int32),
        ],
        scratch_shapes=[pltpu.SMEM((NR,), jnp.int32), pltpu.SMEM((NR,), jnp.int32)],
        name="make_table",
    )(block_ids, weight_rows)


def pick_kernel(wanted_ref, lists_ref, out_ref, order_ref, start_ref, raw, unit, raw_sem, out_sem):
    def load(j):
        return pltpu.make_async_copy(lists_ref.at[j], raw.at[j], raw_sem.at[j])

    def send(i):
        return pltpu.make_async_copy(unit.at[wanted_ref[i]], out_ref.at[i], out_sem.at[i])

    for j in range(CBD):
        load(j).start()

    @pl.loop(0, CBD + 2)
    def _(j):
        start_ref[j] = 0

    @pl.loop(0, ND)
    def _(i):
        j = wanted_ref[i]
        start_ref[j + 1] = start_ref[j + 1] + 1

    @pl.loop(0, CBD)
    def _(j):
        start_ref[j + 1] = start_ref[j + 1] + start_ref[j]

    @pl.loop(0, ND)
    def _(n):
        i = ND - 1 - n
        j = wanted_ref[i]
        at = start_ref[j + 1] - 1
        start_ref[j + 1] = at
        order_ref[at] = i

    start_ref[CBD + 1] = ND

    @pl.loop(0, CBD)
    def _(j):
        load(j).wait()
        unit[j] = unit_rows(raw[j])

        @pl.loop(start_ref[j + 1], start_ref[j + 2])
        def _(n):
            send(order_ref[n]).start()

    @pl.loop(0, ND)
    def _(i):
        send(i).wait()


def pick_lists(centroids, wanted):
    smem = pl.BlockSpec(memory_space=pltpu.SMEM)
    return pl.pallas_call(
        pick_kernel,
        in_specs=[smem, pl.BlockSpec(memory_space=pl.ANY)],
        out_specs=[pl.BlockSpec(memory_space=pl.ANY), smem, smem],
        out_shape=[
            jax.ShapeDtypeStruct((ND, CB, D), BF16),
            jax.ShapeDtypeStruct((ND,), jnp.int32),
            jax.ShapeDtypeStruct((CBD + 2,), jnp.int32),
        ],
        scratch_shapes=[
            pltpu.VMEM((CBD, CB, D), BF16),
            pltpu.VMEM((CBD, CB, D), BF16),
            pltpu.SemaphoreType.DMA((CBD,)),
            pltpu.SemaphoreType.DMA((ND,)),
        ],
        name="pick_lists",
    )(wanted, centroids)


def column_pass(kernel_ref, row_scale, dist_ref, b, parts_ref):
    for k in range(MAXC):
        part = jnp.sum(kernel_ref[b, k] * row_scale, axis=0, keepdims=True)
        d = dist_ref[b * MAXC + k]
        parts_ref[pl.ds(d, 1), :] += part


def spread(parts_ref, out_ref):
    parts = parts_ref[...]
    for r in range(NR):
        out_ref[r] = parts


def prepare(table_ref, spot_ref, same_ref, target_ref):
    rows = [table_ref[r, pl.ds(spot_ref[1], 1), :] for r in range(NR)]
    rows.append(table_ref[spot_ref[0], pl.ds(spot_ref[1], 1), :])
    rows.append(jnp.zeros((CB - NR - 1, CB), F32))
    turned = jnp.transpose(jnp.concatenate(rows, axis=0))
    mine = turned[:ND, NR : NR + 1]
    other = turned[ND : 2 * ND, NR : NR + 1]
    for r in range(NR):
        theirs = turned[:ND, r : r + 1]
        same_ref[0, r] = jnp.broadcast_to(jnp.where(theirs == mine, 1.0, 0.0), (ND, CB))
        same_ref[1, r] = jnp.broadcast_to(jnp.where(theirs == other, 1.0, 0.0), (ND, CB))
    total = jnp.sum(jnp.sum(table_ref[...], axis=0), axis=0, keepdims=True)
    lane = lax.broadcasted_iota(jnp.int32, (1, CB), 1)
    mass = jnp.sum(jnp.where(lane == CB - 1, total, 0.0), axis=1, keepdims=True)
    target_ref[...] = jnp.broadcast_to(mass * (1.0 / K_TOTAL), (8, CB))


def scores_kernel(dist_ref, count_ref, spot_ref, *refs):
    groups_ref, mass_ref, table_ref = refs[:3]
    lists = refs[3 : 3 + MAXC]
    kernel_ref, out_ref, same_ref, target_ref, rows_ref, weight_ref, parts_ref = refs[3 + MAXC :]
    b = pl.program_id(0)
    count = count_ref[b]

    @pl.when(b == 0)
    def _():
        parts_ref[...] = jnp.zeros_like(parts_ref)
        prepare(table_ref, spot_ref, same_ref, target_ref)

    rows = unit_rows(groups_ref[0])
    rows_ref[b] = rows
    for h in range(RB // CB):
        flat = jnp.broadcast_to(mass_ref[pl.ds(b * (RB // CB) + h, 1), :], (CB, CB))
        weight_ref[b, h * CB : (h + 1) * CB, :] = jnp.transpose(flat)

    total = jnp.zeros((RB, CB), F32)
    for k in range(0, MAXC, 2):
        pair = jnp.concatenate([lists[k][0], lists[k + 1][0]], axis=0)
        scores = lax.dot_general(
            rows, pair, (((1,), (1,)), ((), ())), preferred_element_type=F32
        )
        grown = jnp.exp(scores * (BETA / D))
        for n in range(2):
            live = jnp.where(k + n < count, grown[:, n * CB : (n + 1) * CB], 0.0)
            kernel_ref[b, k + n] = live
            total = total + live
    row_scale = weight_ref[b] / jnp.sum(total, axis=1, keepdims=True)
    column_pass(kernel_ref, row_scale, dist_ref, b, parts_ref)

    @pl.when(b == NBD - 1)
    def _():
        spread(parts_ref, out_ref)


def first_pass(dist, counts, spot, groups, weight_rows, table, lists):
    fixed = lambda *shape: pl.BlockSpec(shape, lambda b, d, c, p: (0,) * len(shape))
    list_specs = [
        pl.BlockSpec((1, CB, D), lambda b, d, c, p, k=k: (d[b * MAXC + k], 0, 0))
        for k in range(MAXC)
    ]
    return pl.pallas_call(
        scores_kernel,
        grid_spec=pltpu.PrefetchScalarGridSpec(
            num_scalar_prefetch=3,
            grid=(NBD,),
            in_specs=[pl.BlockSpec((1, RB, D), lambda b, d, c, p: (b, 0, 0)), HELD, HELD]
            + list_specs,
            out_specs=[HELD, fixed(NR, ND, CB), HELD, HELD, HELD, HELD],
            scratch_shapes=[pltpu.VMEM((ND, CB), F32)],
        ),
        out_shape=[
            pltpu.VMEM((NBD, MAXC, RB, CB), F32),
            jax.ShapeDtypeStruct((NR, ND, CB), F32),
            pltpu.VMEM((2, NR, ND, CB), F32),
            pltpu.VMEM((8, CB), F32),
            pltpu.VMEM((NBD, RB, D), BF16),
            pltpu.VMEM((NBD, RB, CB), F32),
        ],
        compiler_params=LIMIT,
        name="scores",
    )(dist, counts, spot, groups, weight_rows, table, *([lists] * MAXC))


def new_scales(got_ref, same_ref, target_ref, scales_ref):
    straight = jnp.zeros((ND, CB), F32)
    crossed = jnp.zeros((ND, CB), F32)
    for r in range(NR):
        got = got_ref[r]
        straight = straight + same_ref[0, r] * got
        crossed = crossed + same_ref[1, r] * got
    even = lax.broadcasted_iota(jnp.int32, (ND, CB), 0) % 2 == 0
    swapped = jnp.where(even, jnp.roll(crossed, -1, axis=0), jnp.roll(crossed, 1, axis=0))
    column = straight + swapped
    target = target_ref[:1]
    scales_ref[...] = target / (column + PRIOR * target)


def row_pass(kernel_ref, weight_ref, scales_ref, dist_ref, b):
    total = jnp.zeros((RB, CB), F32)
    for k in range(MAXC):
        d = dist_ref[b * MAXC + k]
        total = total + kernel_ref[b, k] * scales_ref[pl.ds(d, 1), :]
    return weight_ref[b] / jnp.sum(total, axis=1, keepdims=True)


def turn_kernel(
    dist_ref, kernel_ref, weight_ref, got_ref, same_ref, target_ref, out_ref, scales_ref, parts_ref
):
    b = pl.program_id(0)

    @pl.when(b == 0)
    def _():
        new_scales(got_ref, same_ref, target_ref, scales_ref)
        parts_ref[...] = jnp.zeros_like(parts_ref)

    row_scale = row_pass(kernel_ref, weight_ref, scales_ref, dist_ref, b)
    column_pass(kernel_ref, row_scale, dist_ref, b, parts_ref)

    @pl.when(b == NBD - 1)
    def _():
        spread(parts_ref, out_ref)


def turn(dist, kernel, weights, got, same, target):
    return pl.pallas_call(
        turn_kernel,
        grid_spec=pltpu.PrefetchScalarGridSpec(
            num_scalar_prefetch=1,
            grid=(NBD,),
            in_specs=[HELD] * 5,
            out_specs=HELD,
            scratch_shapes=[pltpu.VMEM((ND, CB), F32), pltpu.VMEM((ND, CB), F32)],
        ),
        out_shape=jax.ShapeDtypeStruct((NR, ND, CB), F32),
        compiler_params=LIMIT,
        name="turn",
    )(dist, kernel, weights, got, same, target)


def final_kernel(
    dist_ref,
    kernel_ref,
    weight_ref,
    rows_ref,
    got_ref,
    same_ref,
    target_ref,
    out_ref,
    scales_ref,
    parts_ref,
    plan_keep,
    order_ref,
    seen_ref,
):
    step = pl.program_id(0)

    @pl.when(step == 0)
    def _():
        new_scales(got_ref, same_ref, target_ref, scales_ref)
        parts_ref[...] = jnp.zeros_like(parts_ref)

        @pl.loop(0, ND)
        def _(d):
            seen_ref[d] = 0

        @pl.loop(0, NBD * MAXC)
        def _(p):
            d = dist_ref[p]
            n = seen_ref[d]
            seen_ref[d] = n + 1
            holder = d // 2
            order_ref[holder * 4 + jnp.where(d % 2 == 0, n, 3 - n)] = p

    @pl.when(step < NBD)
    def _():
        b = step
        row_scale = row_pass(kernel_ref, weight_ref, scales_ref, dist_ref, b)
        for k in range(MAXC):
            d = dist_ref[b * MAXC + k]
            plan = row_scale * kernel_ref[b, k] * scales_ref[pl.ds(d, 1), :]
            parts_ref[pl.ds(d, 1), :] += jnp.sum(plan, axis=0, keepdims=True)
            plan_keep[b * MAXC + k] = jnp.transpose(plan).astype(BF16)

    @pl.when(step >= NBD)
    def _():
        holder = step - NBD
        slots = [order_ref[holder * 4 + n] for n in range(4)]
        plans = [plan_keep[p] for p in slots]
        first = seen_ref[holder * 2]

        def emit(u, chosen):
            left = jnp.concatenate([plans[n] for n in chosen], axis=1)
            right = jnp.concatenate([rows_ref[slots[n] // MAXC] for n in chosen], axis=0)
            total = jnp.dot(left, right, preferred_element_type=F32)
            for c in range(D // 128):
                at = c * USE * CB + u * CB
                out_ref[0, at : at + CB, :] = total[:, c * 128 : (c + 1) * 128].astype(BF16)

        for split in (1, 2, 3):

            @pl.when(first == split)
            def _(split=split):
                emit(0, range(split))
                emit(1, range(split, 4))

        rest = parts_ref[pl.ds(holder * 2, 2), :]
        terms = []
        for _ in range(3):
            piece = rest.astype(BF16).astype(F32)
            terms.append(piece)
            rest = rest - piece
        terms.append(jnp.zeros((10, CB), F32))
        out_ref[0, ROWS_X:, :] = jnp.concatenate(terms, axis=0).astype(BF16)


def final_pass(dist, kernel, weights, rows, got, same, target):
    return pl.pallas_call(
        final_kernel,
        grid_spec=pltpu.PrefetchScalarGridSpec(
            num_scalar_prefetch=1,
            grid=(NBD + NR,),
            in_specs=[HELD] * 6,
            out_specs=pl.BlockSpec((1, ROWS_P, 128), lambda s, d: (jnp.maximum(s - NBD, 0), 0, 0)),
            scratch_shapes=[
                pltpu.VMEM((ND, CB), F32),
                pltpu.VMEM((ND, CB), F32),
                pltpu.VMEM((NBD * MAXC, CB, RB), BF16),
                pltpu.SMEM((NBD * MAXC,), jnp.int32),
                pltpu.SMEM((ND,), jnp.int32),
            ],
        ),
        out_shape=jax.ShapeDtypeStruct((NR, ROWS_P, 128), BF16),
        compiler_params=LIMIT,
        name="final_pass",
    )(dist, kernel, weights, rows, got, same, target)


def merge_kernel(
    wanted_ref, order_ref, start_ref, got_ref, target_ref, out_ref, load_ref, parts, extra, held, in_sem, out_sem
):
    chunks = D // 128

    def fetch(s):
        rows = pl.ds(pl.multiple_of(s * USE * CB, USE * CB), USE * CB)
        return pltpu.make_async_copy(got_ref.at[:, rows, :], parts.at[s], in_sem.at[s])

    def put(s):
        lanes = pl.ds(pl.multiple_of(s * 128, 128), 128)
        return pltpu.make_async_copy(held.at[s], out_ref.at[:, :, lanes], out_sem.at[s])

    for s in range(chunks):
        fetch(s).start()
    tail = pltpu.make_async_copy(got_ref.at[:, pl.ds(ROWS_X, 16), :], extra, in_sem.at[chunks])
    tail.start()

    @pl.loop(0, chunks)
    def _(s):
        fetch(s).wait()
        for j in range(CBD):

            def add(n, total):
                i = order_ref[n]
                at = pl.multiple_of((i % USE) * CB, CB)
                return total + parts[s, i // USE, pl.ds(at, CB), :].astype(F32)

            held[s, j] = lax.fori_loop(
                start_ref[j + 1], start_ref[j + 2], add, jnp.zeros((CB, 128), F32)
            )
        put(s).start()

    tail.wait()
    load_ref[...] = jnp.zeros_like(load_ref)
    for r in range(NR):
        terms = extra[r].astype(F32)
        for u in range(USE):
            mass = terms[u : u + 1] + terms[u + 2 : u + 3] + terms[u + 4 : u + 5]
            load_ref[pl.ds(wanted_ref[r * USE + u], 1), :] += mass
    load_ref[...] = load_ref[...] / target_ref[:1]

    @pl.loop(0, chunks)
    def _(s):
        put(s).wait()


def merge(wanted, order, start, got, target):
    smem = pl.BlockSpec(memory_space=pltpu.SMEM)
    chunks = D // 128
    return pl.pallas_call(
        merge_kernel,
        in_specs=[smem, smem, smem, pl.BlockSpec(memory_space=pl.ANY), HELD],
        out_specs=[pl.BlockSpec(memory_space=pl.ANY), HELD],
        scratch_shapes=[
            pltpu.VMEM((chunks, NR, USE * CB, 128), BF16),
            pltpu.VMEM((NR, 16, 128), BF16),
            pltpu.VMEM((chunks, CBD, CB, 128), F32),
            pltpu.SemaphoreType.DMA((chunks + 1,)),
            pltpu.SemaphoreType.DMA((chunks,)),
        ],
        out_shape=[
            jax.ShapeDtypeStruct((CBD, CB, D), F32),
            jax.ShapeDtypeStruct((CBD, CB), F32),
        ],
        name="merge",
    )(wanted, order, start, got, target)


def exchange(values):
    return lax.all_to_all(values, "rows", split_axis=0, concat_axis=0, tiled=True)


def body(groups, centroids, row_weight, block_ids, block_counts):
    weight_rows = row_weight.reshape(NBD * RB // CB, CB)
    table, dist = make_table(block_ids, weight_rows)
    me = lax.axis_index("rows")
    side = lax.axis_index("cents")
    spot = jnp.stack([me, side]).astype(jnp.int32)
    table, spot = lax.optimization_barrier((table, spot))
    tables = lax.all_to_all(
        table.reshape(DEVICES, 1, CB), ("rows", "cents"), split_axis=0, concat_axis=0, tiled=True
    ).reshape(NR, NC, CB)
    wanted = lax.dynamic_slice(tables, (0, spot[1], spot[0] * USE), (NR, 1, USE))
    wanted = wanted.reshape(-1).astype(jnp.int32)
    picked, order, start = pick_lists(centroids.reshape(CBD, CB, D), wanted)
    lists = exchange(picked.reshape(NR, USE * CB, D)).reshape(ND, CB, D)

    groups = groups.reshape(NBD, RB, D)
    kernel, parts, same, target, rows, weights = first_pass(
        dist, block_counts, spot, groups, weight_rows, tables, lists
    )
    got = exchange(parts)
    for _ in range(ITERS - 1):
        got = exchange(turn(dist, kernel, weights, got, same, target))
    sums = final_pass(dist, kernel, weights, rows, got, same, target)
    totals, load = merge(wanted, order, start, exchange(sums), target)
    return totals.reshape(-1, D), load.reshape(-1)


def solution(mesh):
    placed = (
        P(("rows", "cents"), None),
        P(("rows", "cents"), None),
        P(("rows", "cents")),
        P(("rows", "cents"), None),
        P(("rows", "cents")),
    )
    return jax.shard_map(
        body,
        mesh=mesh,
        in_specs=placed,
        out_specs=(P(("rows", "cents"), None), P(("rows", "cents"))),
        check_vma=False,
    )
```

time: 348 us -> 310 us (0.89)
  Pallas kernels: 80.5 us -> 53.3 us
  blocking collectives: 240 us -> 234 us
  local copies, waits for them, and re-layouts: 6.08 us -> 1.32 us
  waiting for transfers between devices: 2.03 us -> 6.06 us
  other arithmetic: 3.98 us -> 0.18 us
    pallas_call x5, Pallas kernels: 43.3 us -> 23.1 us  [the longest x1 9.61 us: merge(): pl.pallas_call(merge_kernel, in_specs=[smem, smem, smem, pl.BlockSpec(mem...]
    all_to_all x1, waiting for transfers between devices: 0.01 us -> 6.06 us  [body(): lax.all_to_all(table.reshape(DEVICES, 1, CB), ('rows', 'cents'), split_ax...]
    all_to_all x5, blocking collectives: 240 us -> 234 us  [exchange(): lax.all_to_all(values, 'rows', split_axis=0, concat_axis=0, tiled=True)]
    pallas_call x1, Pallas kernels: 21.4 us -> 16 us  [final_pass(): pl.pallas_call(final_kernel, grid_spec=pltpu.PrefetchScalarGridSpec(num_s...]
    ppermute x3 -> x0, starting transfers between devices: 5.01 us -> none  [body(): mass = mass + lax.ppermute(mass, 'cents', [(i, i ^ bit) for i in range(NC)])]
    broadcast_in_dim x6 -> x0, local copies, waits for them, and re-layouts: 4.39 us -> none  [the longest x2 2.07 us: body(): weights = jnp.broadcast_to(row_weight.reshape(NBD, RB, 1), (NBD, RB, CB))]
  transfers between devices with their start and end apart: 4 -> 1, of which waited for: 1 -> 1; matrix products, arithmetic and copies ran while one was open for 1% -> 0% of each run, Pallas kernels for 4% -> 0%
where the time goes in v2:
time: 310 us; the launch traced here: 309 us
  blocking collectives  234 us (75%)
  Pallas kernels  53.3 us (17%)
  starting transfers between devices  11.2 us (4%)
  waiting for transfers between devices  6.06 us (2%)
  between operations  3.29 us (1%)
    all_to_all x5, blocking collectives, exchange(): lax.all_to_all(values, 'rows', split_axis=0, concat_axis=0, tiled=True)  234 us
    pallas_call x1, Pallas kernels, final_pass(): pl.pallas_call(final_kernel, grid_spec=pltpu.PrefetchScalarGridSpec(num_s...  16 us
    pallas_call x1, Pallas kernels, first_pass(): pl.pallas_call(scores_kernel, grid_spec=pltpu.PrefetchScalarGridSpec(num_...  14.1 us
    all_to_all x1, starting transfers between devices, body(): lax.all_to_all(table.reshape(DEVICES, 1, CB), ('rows', 'cents'), split_ax...  11.2 us
    pallas_call x1, Pallas kernels, merge(): pl.pallas_call(merge_kernel, in_specs=[smem, smem, smem, pl.BlockSpec(mem...  9.61 us
  transfers between devices with their start and end apart: 1, of which 1 were waited for; matrix products, arithmetic and copies ran while one was open for 0% of the time, Pallas kernels for 0%

profile of v2, /device:TPU:0, one launch (start us, length us, event | category | flops | bytes accessed | tf_op | source)
XLA Modules:
  0.0 309.5 jit_solution(7451424203659033807)
XLA Ops:
  0.6 0.1 pad_add_fusion.spot_ref
  0.7 2.8 make_table.1
  3.5 11.2 %all-to-all-start = ((f32[128,1,128]{2,1,0:T(1,128)}), f32[128,1,128]{2,1,0:T(1,128)S(1)}, u32[]{:S(2)}, u32[]{:S(2)}) async-start(f32[128,1,128]{2,1,0:T(1,128)} %bitcast.30), calls=%async_computation | async-start | bytes 131072 | tf_op jit(solution)/shard_map/all_to_all | solution.py:487
  14.7 0.6 fusion
  17.9 6.1 %all-to-all-done = f32[128,1,128]{2,1,0:T(1,128)S(1)} async-done(((f32[128,1,128]{2,1,0:T(1,128)}), f32[128,1,128]{2,1,0:T(1,128)S(1)}, u32[]{:S(2)}, u32[]{:S(2)}) %all-to-all-start) | async-done | bytes 65568 | tf_op jit(solution)/shard_map/all_to_all | solution.py:487
  23.9 0.1 convert_reduce_fusion
  24.0 0.7 convert_element_type.6.wanted_ref
  24.7 6.1 %pick_lists.1 = (bf16[32,128,1024]{2,1,0:T(8,128)(2,1)}, s32[32]{0:T(128)}, s32[18]{0:T(128)}) custom-call(s32[32]{0:T(128)} %convert_element_type.6.wanted_ref, bf16[16,128,1024]{2,1,0:T(8,128)(2,1)} %bitcast.28), custom_call_target="tpu_custom_call" | custom-call | tf_op jit(solution)/shard_map/pick_lists/pallas_call | solution.py:138
  30.8 0.0 copy-start.1
  30.8 0.0 copy-start.2
  30.8 0.0 copy-start.3
  30.9 101.0 %all_to_all.30 = bf16[16,256,1024]{2,1,0:T(8,128)(2,1)} all-to-all(bf16[16,256,1024]{2,1,0:T(8,128)(2,1)} %bitcast.27), channel_id=1, replica_groups=mesh['rows'=16,'cents'=8] {'rows'}, dimensions={0} | all-to-all | bytes 16777216 | tf_op jit(solution)/shard_map/all_to_all | solution.py:477
  131.8 0.0 copy-done.1
  131.8 0.0 copy-done.2
  131.8 14.1 %scores.1 = (f32[8,8,256,128]{3,2,1,0:T(8,128)S(1)}, f32[16,32,128]{2,1,0:T(8,128)S(1)}, f32[2,16,32,128]{3,2,1,0:T(8,128)S(1)}, f32[8,128]{1,0:T(8,128)S(1)}, b...) custom-call(s32[64]{0:T(128)S(1)} %copy-done.2, s32[8]{0:T(128)S(1)} %copy-done.3, ...), custom_call_target="tpu_custom_call" | custom-call | tf_op jit(solution)/shard_map/scores/pallas_call | solution.py:230
  146.0 0.0 copy-start
  146.0 11.6 %all_to_all.31.got_ref = f32[16,32,128]{2,1,0:T(8,128)S(1)} all-to-all(f32[16,32,128]{2,1,0:T(8,128)S(1)} %get-tuple-element.27), channel_id=1, replica_groups=mesh['rows'=16,'cents'=8] {'rows'}, dimensions={0} | all-to-all | bytes 524288 | tf_op jit(solution)/shard_map/all_to_all | solution.py:477
  157.6 2.3 turn.2
  159.9 11.6 %all_to_all.32.got_ref = f32[16,32,128]{2,1,0:T(8,128)S(1)} all-to-all(f32[16,32,128]{2,1,0:T(8,128)S(1)} %turn.2), channel_id=1, replica_groups=mesh['rows'=16,'cents'=8] {'rows'}, dimensions={0} | all-to-all | bytes 524288 | tf_op jit(solution)/shard_map/all_to_all | solution.py:477
  171.5 2.3 turn.3
  173.8 11.6 %all_to_all.33.got_ref = f32[16,32,128]{2,1,0:T(8,128)S(1)} all-to-all(f32[16,32,128]{2,1,0:T(8,128)S(1)} %turn.3), channel_id=1, replica_groups=mesh['rows'=16,'cents'=8] {'rows'}, dimensions={0} | all-to-all | bytes 524288 | tf_op jit(solution)/shard_map/all_to_all | solution.py:477
  185.4 16.0 %final_pass.1 = bf16[16,2064,128]{2,1,0:T(8,128)(2,1)} custom-call(s32[64]{0:T(128)S(1)} %copy-done.2, f32[8,8,256,128]{3,2,1,0:T(8,128)S(1)} %get-tuple-element.24.kernel_ref, f32[8,256,128]{2,1,0:T(8,128)S(1)} %get-tuple-element.25.weight_ref, bf16[8,256,1024]{2,1,0:T(8,128)(2,1)S(1)} %get-tuple-element.26.rows_ref, ...), custom_call_target="tpu_custom_call" | custom-call | tf_op jit(solution)/shard_map/final_pass/pallas_call | solution.py:386
  201.5 98.4 %all_to_all.34.got_ref = bf16[16,2064,128]{2,1,0:T(8,128)(2,1)} all-to-all(bf16[16,2064,128]{2,1,0:T(8,128)(2,1)} %final_pass.1), channel_id=1, replica_groups=mesh['rows'=16,'cents'=8] {'rows'}, dimensions={0} | all-to-all | bytes 16908288 | tf_op jit(solution)/shard_map/all_to_all | solution.py:477
  299.9 9.6 %merge.1 = (f32[16,128,1024]{2,1,0:T(8,128)}, f32[16,128]{1,0:T(8,128)}) custom-call(s32[32]{0:T(128)} %convert_element_type.6.wanted_ref, s32[32]{0:T(128)} %get-tuple-element.20.order_ref, s32[18]{0:T(128)} %get-tuple-element.21.start_ref, bf16[16,2064,128]{2,1,0:T(8,128)(2,1)} %all_to_all.34.got_ref, f32[8,128]{1,0:T(8,128)} %copy-done), custom_call_target="tpu_custom_call" | custom-call | tf_op jit(solution)/shard_map/merge/pallas_call | solution.py:457
  (2 shorter events, 0.0 us)
Async XLA Ops:
  3.5 20.4 %all-to-all-start = ((f32[128,1,128]{2,1,0:T(1,128)}), f32[128,1,128]{2,1,0:T(1,128)S(1)}, u32[]{:S(2)}, u32[]{:S(2)}) async-start(f32[128,1,128]{2,1,0:T(1,128)} %bitcast.30), calls=%async_computation | async-start | bytes 131072 | tf_op jit(solution)/shard_map/all_to_all | solution.py:487
  30.8 101.0 %copy-start.1 = (f32[2048]{0:T(1024)S(1)}, f32[2048]{0:T(1024)}, u32[]{:S(2)}) copy-start(f32[2048]{0:T(1024)} %param.7) | copy-start | bytes 24580
  30.8 101.0 %copy-start.2 = (s32[64]{0:T(128)S(1)}, s32[64]{0:T(128)}, u32[]{:S(2)}) copy-start(s32[64]{0:T(128)} %get-tuple-element.22.dist_ref) | copy-start | bytes 772
  30.8 101.0 %copy-start.3 = (s32[8]{0:T(128)S(1)}, s32[8]{0:T(128)}, u32[]{:S(2)}) copy-start(s32[8]{0:T(128)} %count_ref.1) | copy-start | bytes 100
  146.0 39.4 %copy-start = (f32[8,128]{1,0:T(8,128)}, f32[8,128]{1,0:T(8,128)S(1)}, u32[]{:S(2)}) copy-start(f32[8,128]{1,0:T(8,128)S(1)} %get-tuple-element.29.target_ref) | copy-start | bytes 12292

commit v3 on v2

v3 whole, which is shorter than its diff:
```python
import jax
import jax.numpy as jnp
from jax import lax
from jax.experimental import pallas as pl
from jax.experimental.pallas import tpu as pltpu
from jax.sharding import PartitionSpec as P

D = 1024
RB = 256
CB = 128
MAXC = 8
USE = 2
ITERS = 3
NBD = 8
CBD = 16
NR = 16
NC = 8
ND = NR * USE
DEVICES = NR * NC
K_TOTAL = DEVICES * CBD * CB
ROWS_X = USE * CB * (D // 128)
ROWS_P = ROWS_X + 16

BETA = 32.0
EPSILON = 1e-06
PRIOR = 0.25
F32 = jnp.float32
BF16 = jnp.bfloat16
HELD = pl.BlockSpec(memory_space=pltpu.VMEM)
LIMIT = pltpu.CompilerParams(vmem_limit_bytes=20 << 20)


def unit_rows(values):
    widened = values.astype(F32)
    mean = jnp.sum(widened * widened, axis=-1, keepdims=True) * (1.0 / D)
    return (widened * lax.rsqrt(mean + EPSILON)).astype(BF16)


def table_kernel(ids_ref, weight_ref, table_ref, dist_ref, low_ref, high_ref):
    for o in range(NR):
        low_ref[o] = -1
        high_ref[o] = -1

    @pl.loop(0, NBD)
    def _(b):
        for k in range(MAXC):
            number = ids_ref[b, k]
            holder = number // (CBD * NC)
            local = number % CBD
            seen = low_ref[holder]
            low = jnp.where(seen < 0, local, seen)
            low_ref[holder] = low
            rank = jnp.where(local != low, 1, 0)
            high_ref[holder] = jnp.where(rank == 1, local, high_ref[holder])
            dist_ref[b * MAXC + k] = holder * USE + rank

    weight = jnp.sum(jnp.sum(weight_ref[...], axis=0, keepdims=True), axis=1, keepdims=True)
    lane = lax.broadcasted_iota(jnp.int32, (1, CB), 1)
    numbers = jnp.zeros((1, CB), jnp.int32)
    for o in range(NR):
        low = low_ref[o]
        high = high_ref[o]
        is_low = (lane == USE * o) | (lane == ND + USE * o + 1)
        is_high = (lane == USE * o + 1) | (lane == ND + USE * o)
        numbers = jnp.where(is_low, low, jnp.where(is_high, high, numbers))
    row = jnp.where(lane < 2 * ND, numbers.astype(F32), jnp.broadcast_to(weight, (1, CB)))
    table_ref[...] = jnp.broadcast_to(row, (DEVICES, CB))


def make_table(block_ids, weight_rows):
    return pl.pallas_call(
        table_kernel,
        in_specs=[pl.BlockSpec(memory_space=pltpu.SMEM), HELD],
        out_specs=[HELD, pl.BlockSpec(memory_space=pltpu.SMEM)],
        out_shape=[
            jax.ShapeDtypeStruct((DEVICES, CB), F32),
            jax.ShapeDtypeStruct((NBD * MAXC,), jnp.int32),
        ],
        scratch_shapes=[pltpu.SMEM((NR,), jnp.int32), pltpu.SMEM((NR,), jnp.int32)],
        name="make_table",
    )(block_ids, weight_rows)


def unit_kernel(lists_ref, groups_ref, unit_ref, rows_ref, raw, made, in_sem, out_sem):
    def span(n):
        return pl.ds(pl.multiple_of(n * CB, CB), CB)

    def load(source, n, at):
        return pltpu.make_async_copy(source.at[span(n)], raw.at[at], in_sem.at[at])

    def store(target, n, at):
        return pltpu.make_async_copy(made.at[at], target.at[span(n)], out_sem.at[at])

    pairs = ((lists_ref, unit_ref, 0), (groups_ref, rows_ref, CBD))
    for source, _, base in pairs:
        for n in range(CBD):
            load(source, n, base + n).start()
    for source, target, base in pairs:

        @pl.loop(0, CBD)
        def _(n, source=source, target=target, base=base):
            load(source, n, base + n).wait()
            made[base + n] = unit_rows(raw[base + n])
            store(target, n, base + n).start()

    for _, target, base in pairs:

        @pl.loop(0, CBD)
        def _(n, target=target, base=base):
            store(target, n, base + n).wait()


def unit_vectors(centroids, groups):
    far = pl.BlockSpec(memory_space=pl.ANY)
    return pl.pallas_call(
        unit_kernel,
        in_specs=[far, far],
        out_specs=[far, far],
        out_shape=[jax.ShapeDtypeStruct(centroids.shape, BF16), jax.ShapeDtypeStruct(groups.shape, BF16)],
        scratch_shapes=[
            pltpu.VMEM((2 * CBD, CB, D), BF16),
            pltpu.VMEM((2 * CBD, CB, D), BF16),
            pltpu.SemaphoreType.DMA((2 * CBD,)),
            pltpu.SemaphoreType.DMA((2 * CBD,)),
        ],
        cost_estimate=pl.CostEstimate(flops=1 << 24, bytes_accessed=1 << 24, transcendentals=1 << 12),
        name="unit_vectors",
    )(centroids, groups)


def prepare(rows, mine, tables_ref, same_ref, target_ref):
    filler = jnp.zeros((CB - NR - 1, CB), F32)
    turned = jnp.transpose(jnp.concatenate([rows, mine, filler], axis=0))
    here = turned[:ND, NR : NR + 1]
    other = turned[ND : 2 * ND, NR : NR + 1]
    for r in range(NR):
        theirs = turned[:ND, r : r + 1]
        same_ref[0, r] = jnp.broadcast_to(jnp.where(theirs == here, 1.0, 0.0), (ND, CB))
        same_ref[1, r] = jnp.broadcast_to(jnp.where(theirs == other, 1.0, 0.0), (ND, CB))
    total = jnp.sum(jnp.sum(tables_ref[...], axis=0), axis=0, keepdims=True)
    lane = lax.broadcasted_iota(jnp.int32, (1, CB), 1)
    mass = jnp.sum(jnp.where(lane == CB - 1, total, 0.0), axis=1, keepdims=True)
    target_ref[...] = jnp.broadcast_to(mass * (1.0 / K_TOTAL), (8, CB))


def pick_kernel(
    tables_ref,
    table_ref,
    lists_ref,
    out_ref,
    wanted_ref,
    same_ref,
    target_ref,
    numbers,
    scalars,
    unit,
    in_sem,
    move_sem,
):
    me = lax.axis_index("rows")
    side = lax.axis_index("cents")

    def load(j):
        return pltpu.make_async_copy(lists_ref.at[j], unit.at[j], in_sem.at[j])

    for j in range(CBD):
        load(j).start()
    rows = jnp.concatenate([tables_ref[r, pl.ds(side, 1), :] for r in range(NR)], axis=0)
    numbers[...] = rows.astype(jnp.int32)
    move = pltpu.make_async_copy(numbers, scalars, move_sem)
    move.start()
    prepare(rows, table_ref[:1], tables_ref, same_ref, target_ref)
    move.wait()
    for j in range(CBD):
        load(j).wait()

    @pl.loop(0, NR)
    def _(r):
        for u in range(USE):
            j = scalars[r, me * USE + u]
            wanted_ref[r * USE + u] = j
            out_ref[r * USE + u] = unit[j]


def pick_lists(tables, table, unit):
    return pl.pallas_call(
        pick_kernel,
        in_specs=[HELD, HELD, pl.BlockSpec(memory_space=pl.ANY)],
        out_specs=[HELD, pl.BlockSpec(memory_space=pltpu.SMEM), HELD, HELD],
        out_shape=[
            pltpu.VMEM((ND, CB, D), BF16),
            jax.ShapeDtypeStruct((ND,), jnp.int32),
            pltpu.VMEM((2, NR, ND, CB), F32),
            pltpu.VMEM((8, CB), F32),
        ],
        scratch_shapes=[
            pltpu.VMEM((NR, CB), jnp.int32),
            pltpu.SMEM((NR, CB), jnp.int32),
            pltpu.VMEM((CBD, CB, D), BF16),
            pltpu.SemaphoreType.DMA((CBD,)),
            pltpu.SemaphoreType.DMA,
        ],
        compiler_params=pltpu.CompilerParams(vmem_limit_bytes=54 << 20),
        name="pick_lists",
    )(tables, table, unit)


def column_pass(kernel_ref, row_scale, dist_ref, b, parts_ref):
    for k in range(MAXC):
        part = jnp.sum(kernel_ref[b, k] * row_scale, axis=0, keepdims=True)
        d = dist_ref[b * MAXC + k]
        parts_ref[pl.ds(d, 1), :] += part


def spread(parts_ref, out_ref):
    parts = parts_ref[...]
    for r in range(NR):
        out_ref[r] = parts


STEP = 2


def scores_kernel(dist_ref, count_ref, *refs):
    rows_ref, mass_ref, lists_ref, kernel_ref, out_ref, weight_ref, parts_ref = refs
    step = pl.program_id(0)

    @pl.when(step == 0)
    def _():
        parts_ref[...] = jnp.zeros_like(parts_ref)

    for n in range(STEP):
        b = step * STEP + n
        count = count_ref[b]
        rows = rows_ref[b]
        halves = []
        for h in range(RB // CB):
            flat = jnp.broadcast_to(mass_ref[pl.ds(b * (RB // CB) + h, 1), :], (CB, CB))
            halves.append(jnp.transpose(flat))
        weight = jnp.concatenate(halves, axis=0)
        weight_ref[b] = weight
        total = jnp.zeros((RB, CB), F32)
        for k in range(0, MAXC, 2):
            named = [dist_ref[b * MAXC + k + m] for m in range(2)]
            pair = jnp.concatenate([lists_ref[d] for d in named], axis=0)
            scores = lax.dot_general(
                rows, pair, (((1,), (1,)), ((), ())), preferred_element_type=F32
            )
            grown = jnp.exp(scores * (BETA / D))
            for m in range(2):
                live = jnp.where(k + m < count, grown[:, m * CB : (m + 1) * CB], 0.0)
                kernel_ref[b, k + m] = live
                total = total + live
        row_scale = weight / jnp.sum(total, axis=1, keepdims=True)
        column_pass(kernel_ref, row_scale, dist_ref, b, parts_ref)

    @pl.when(step == NBD // STEP - 1)
    def _():
        spread(parts_ref, out_ref)


def first_pass(dist, counts, rows, weight_rows, lists):
    return pl.pallas_call(
        scores_kernel,
        grid_spec=pltpu.PrefetchScalarGridSpec(
            num_scalar_prefetch=2,
            grid=(NBD // STEP,),
            in_specs=[HELD] * 3,
            out_specs=[HELD] * 3,
            scratch_shapes=[pltpu.VMEM((ND, CB), F32)],
        ),
        out_shape=[
            pltpu.VMEM((NBD, MAXC, RB, CB), F32),
            jax.ShapeDtypeStruct((NR, ND, CB), F32),
            pltpu.VMEM((NBD, RB, CB), F32),
        ],
        compiler_params=LIMIT,
        name="scores",
    )(dist, counts, rows, weight_rows, lists)


def new_scales(got_ref, same_ref, target_ref, scales_ref):
    straight = jnp.zeros((ND, CB), F32)
    crossed = jnp.zeros((ND, CB), F32)
    for r in range(NR):
        got = got_ref[r]
        straight = straight + same_ref[0, r] * got
        crossed = crossed + same_ref[1, r] * got
    even = lax.broadcasted_iota(jnp.int32, (ND, CB), 0) % 2 == 0
    swapped = jnp.where(even, jnp.roll(crossed, -1, axis=0), jnp.roll(crossed, 1, axis=0))
    column = straight + swapped
    target = target_ref[:1]
    scales_ref[...] = target / (column + PRIOR * target)


def row_pass(kernel_ref, weight_ref, scales_ref, dist_ref, b):
    total = jnp.zeros((RB, CB), F32)
    for k in range(MAXC):
        d = dist_ref[b * MAXC + k]
        total = total + kernel_ref[b, k] * scales_ref[pl.ds(d, 1), :]
    return weight_ref[b] / jnp.sum(total, axis=1, keepdims=True)


def turn_kernel(
    dist_ref, kernel_ref, weight_ref, got_ref, same_ref, target_ref, out_ref, scales_ref, parts_ref
):
    b = pl.program_id(0)

    @pl.when(b == 0)
    def _():
        new_scales(got_ref, same_ref, target_ref, scales_ref)
        parts_ref[...] = jnp.zeros_like(parts_ref)

    row_scale = row_pass(kernel_ref, weight_ref, scales_ref, dist_ref, b)
    column_pass(kernel_ref, row_scale, dist_ref, b, parts_ref)

    @pl.when(b == NBD - 1)
    def _():
        spread(parts_ref, out_ref)


def turn(dist, kernel, weights, got, same, target):
    return pl.pallas_call(
        turn_kernel,
        grid_spec=pltpu.PrefetchScalarGridSpec(
            num_scalar_prefetch=1,
            grid=(NBD,),
            in_specs=[HELD] * 5,
            out_specs=HELD,
            scratch_shapes=[pltpu.VMEM((ND, CB), F32), pltpu.VMEM((ND, CB), F32)],
        ),
        out_shape=jax.ShapeDtypeStruct((NR, ND, CB), F32),
        compiler_params=LIMIT,
        name="turn",
    )(dist, kernel, weights, got, same, target)


def final_kernel(
    dist_ref,
    kernel_ref,
    weight_ref,
    rows_ref,
    got_ref,
    same_ref,
    target_ref,
    out_ref,
    scales_ref,
    parts_ref,
    plan_keep,
    order_ref,
    seen_ref,
):
    step = pl.program_id(0)

    @pl.when(step == 0)
    def _():
        new_scales(got_ref, same_ref, target_ref, scales_ref)
        parts_ref[...] = jnp.zeros_like(parts_ref)

        for d in range(ND):
            seen_ref[d] = 0

    @pl.when(step < NBD)
    def _():
        b = step
        row_scale = row_pass(kernel_ref, weight_ref, scales_ref, dist_ref, b)
        for k in range(MAXC):
            d = dist_ref[b * MAXC + k]
            plan = row_scale * kernel_ref[b, k] * scales_ref[pl.ds(d, 1), :]
            parts_ref[pl.ds(d, 1), :] += jnp.sum(plan, axis=0, keepdims=True)
            plan_keep[b * MAXC + k] = jnp.transpose(plan.astype(BF16))
            n = seen_ref[d]
            seen_ref[d] = n + 1
            order_ref[d // 2 * 4 + jnp.where(d % 2 == 0, n, 3 - n)] = b * MAXC + k

    @pl.when(step >= NBD)
    def _():
        holder = step - NBD
        slots = [order_ref[holder * 4 + n] for n in range(4)]
        plans = [plan_keep[p] for p in slots]
        first = seen_ref[holder * 2]

        def emit(u, chosen):
            left = jnp.concatenate([plans[n] for n in chosen], axis=1)
            right = jnp.concatenate([rows_ref[slots[n] // MAXC] for n in chosen], axis=0)
            total = jnp.dot(left, right, preferred_element_type=F32)
            for c in range(D // 128):
                at = c * USE * CB + u * CB
                out_ref[holder, at : at + CB, :] = total[:, c * 128 : (c + 1) * 128].astype(BF16)

        for split in (1, 2, 3):

            @pl.when(first == split)
            def _(split=split):
                emit(0, range(split))
                emit(1, range(split, 4))

        rest = parts_ref[pl.ds(holder * 2, 2), :]
        terms = []
        for _ in range(3):
            piece = rest.astype(BF16).astype(F32)
            terms.append(piece)
            rest = rest - piece
        terms.append(jnp.zeros((10, CB), F32))
        out_ref[holder, ROWS_X:, :] = jnp.concatenate(terms, axis=0).astype(BF16)


def final_pass(dist, kernel, weights, rows, got, same, target):
    return pl.pallas_call(
        final_kernel,
        grid_spec=pltpu.PrefetchScalarGridSpec(
            num_scalar_prefetch=1,
            grid=(NBD + NR,),
            in_specs=[HELD] * 6,
            out_specs=HELD,
            scratch_shapes=[
                pltpu.VMEM((ND, CB), F32),
                pltpu.VMEM((ND, CB), F32),
                pltpu.VMEM((NBD * MAXC, CB, RB), BF16),
                pltpu.SMEM((NBD * MAXC,), jnp.int32),
                pltpu.SMEM((ND,), jnp.int32),
            ],
        ),
        out_shape=pltpu.VMEM((NR, ROWS_P, 128), BF16),
        compiler_params=LIMIT,
        name="final_pass",
    )(dist, kernel, weights, rows, got, same, target)


def merge_kernel(
    wanted_ref, got_ref, target_ref, out_ref, load_ref, held, order_ref, start_ref, out_sem
):
    chunks = D // 128

    def put(s):
        lanes = pl.ds(pl.multiple_of(s * 128, 128), 128)
        return pltpu.make_async_copy(held.at[s], out_ref.at[:, :, lanes], out_sem.at[s])

    for j in range(CBD + 2):
        start_ref[j] = 0

    @pl.loop(0, ND)
    def _(i):
        j = wanted_ref[i]
        start_ref[j + 1] = start_ref[j + 1] + 1

    @pl.loop(0, CBD)
    def _(j):
        begin = start_ref[j]
        count = start_ref[j + 1]
        start_ref[j + 1] = begin + count

        @pl.when(count == 0)
        def _():
            for s in range(chunks):
                held[s, j] = jnp.zeros((CB, 128), F32)

    @pl.loop(0, ND)
    def _(i):
        j = wanted_ref[i]
        at = start_ref[j]
        start_ref[j] = at + 1
        order_ref[at] = i

    @pl.loop(0, chunks)
    def _(s):
        total = jnp.zeros((CB, 128), F32)
        last = -1
        for n in range(ND):
            i = order_ref[n]
            j = wanted_ref[i]
            at = pl.multiple_of(s * (USE * CB) + (i % USE) * CB, CB)
            part = got_ref[i // USE, pl.ds(at, CB), :].astype(F32)
            total = part + jnp.where(j == last, total, 0.0)
            held[s, j] = total
            last = j
        put(s).start()

    load_ref[...] = jnp.zeros_like(load_ref)
    for r in range(NR):
        terms = got_ref[r, ROWS_X:, :].astype(F32)
        for u in range(USE):
            mass = terms[u : u + 1] + terms[u + 2 : u + 3] + terms[u + 4 : u + 5]
            load_ref[pl.ds(wanted_ref[r * USE + u], 1), :] += mass
    load_ref[...] = load_ref[...] / target_ref[:1]

    @pl.loop(0, chunks)
    def _(s):
        put(s).wait()


def merge(wanted, got, target):
    chunks = D // 128
    return pl.pallas_call(
        merge_kernel,
        in_specs=[pl.BlockSpec(memory_space=pltpu.SMEM), HELD, HELD],
        out_specs=[pl.BlockSpec(memory_space=pl.ANY), HELD],
        scratch_shapes=[
            pltpu.VMEM((chunks, CBD, CB, 128), F32),
            pltpu.SMEM((ND,), jnp.int32),
            pltpu.SMEM((CBD + 2,), jnp.int32),
            pltpu.SemaphoreType.DMA((chunks,)),
        ],
        out_shape=[
            jax.ShapeDtypeStruct((CBD, CB, D), F32),
            jax.ShapeDtypeStruct((CBD, CB), F32),
        ],
        compiler_params=LIMIT,
        name="merge",
    )(wanted, got, target)


def exchange(values):
    return lax.all_to_all(values, "rows", split_axis=0, concat_axis=0, tiled=True)


def body(groups, centroids, row_weight, block_ids, block_counts):
    weight_rows = row_weight.reshape(NBD * RB // CB, CB)
    table, dist = make_table(block_ids, weight_rows)
    tables = lax.all_to_all(
        table.reshape(DEVICES, 1, CB), ("rows", "cents"), split_axis=0, concat_axis=0, tiled=True
    ).reshape(NR, NC, CB)
    unit, rows = unit_vectors(centroids, groups)
    picked, wanted, same, target = pick_lists(
        tables, table, unit.reshape(CBD, CB, D)
    )
    rows = rows.reshape(NBD, RB, D)
    lists = exchange(picked.reshape(NR, USE * CB, D)).reshape(ND, CB, D)

    kernel, parts, weights = first_pass(dist, block_counts, rows, weight_rows, lists)
    got = exchange(parts)
    for _ in range(ITERS - 1):
        got = exchange(turn(dist, kernel, weights, got, same, target))
    sums = final_pass(dist, kernel, weights, rows, got, same, target)
    totals, load = merge(wanted, exchange(sums), target)
    return totals.reshape(-1, D), load.reshape(-1)


def solution(mesh):
    placed = (
        P(("rows", "cents"), None),
        P(("rows", "cents"), None),
        P(("rows", "cents")),
        P(("rows", "cents"), None),
        P(("rows", "cents")),
    )
    return jax.shard_map(
        body,
        mesh=mesh,
        in_specs=placed,
        out_specs=(P(("rows", "cents"), None), P(("rows", "cents"))),
        check_vma=False,
    )
```

time: 310 us -> 293 us (0.945)
  Pallas kernels: 53.3 us -> 45.3 us
  waiting for transfers between devices: 6.06 us -> 2.24 us
    pallas_call x1, Pallas kernels: 14.1 us -> 7.06 us  [first_pass(): pl.pallas_call(scores_kernel, grid_spec=pltpu.PrefetchScalarGridSpec(num_...]
    pallas_call x1, Pallas kernels: 16 us -> 11.9 us  [final_pass(): pl.pallas_call(final_kernel, grid_spec=pltpu.PrefetchScalarGridSpec(num_s...]
    all_to_all x1, waiting for transfers between devices: 6.06 us -> 2.24 us  [body(): lax.all_to_all(table.reshape(DEVICES, 1, CB), ('rows', 'cents'), split_ax...]
    pallas_call x2 -> x3, Pallas kernels: 15.7 us -> 19.5 us  [the longest x1 7.35 us: merge(): pl.pallas_call(merge_kernel, in_specs=[pl.BlockSpec(memory_space=pltpu.SM...]
  transfers between devices with their start and end apart: 1 -> 1, of which waited for: 1 -> 1; matrix products, arithmetic and copies ran while one was open for 0% -> 0% of each run, Pallas kernels for 0% -> 2%
where the time goes in v3:
time: 293 us; the launch traced here: 292 us
  blocking collectives  232 us (79%)
  Pallas kernels  45.3 us (15%)
  starting transfers between devices  11.2 us (4%)
    all_to_all x5, blocking collectives, exchange(): lax.all_to_all(values, 'rows', split_axis=0, concat_axis=0, tiled=True)  232 us
    pallas_call x1, Pallas kernels, final_pass(): pl.pallas_call(final_kernel, grid_spec=pltpu.PrefetchScalarGridSpec(num_s...  11.9 us
    all_to_all x1, starting transfers between devices, body(): lax.all_to_all(table.reshape(DEVICES, 1, CB), ('rows', 'cents'), split_ax...  11.2 us
    pallas_call x1, Pallas kernels, merge(): pl.pallas_call(merge_kernel, in_specs=[pl.BlockSpec(memory_space=pltpu.SM...  7.35 us
    pallas_call x1, Pallas kernels, unit_vectors(): pl.pallas_call(unit_kernel, in_specs=[far, far], out_specs=[far, far], ou...  7.07 us
    pallas_call x1, Pallas kernels, first_pass(): pl.pallas_call(scores_kernel, grid_spec=pltpu.PrefetchScalarGridSpec(num_...  7.06 us
  transfers between devices with their start and end apart: 1, of which 1 were waited for; matrix products, arithmetic and copies ran while one was open for 0% of the time, Pallas kernels for 2%

profile of v3, /device:TPU:0, one launch (start us, length us, event | category | flops | bytes accessed | tf_op | source)
XLA Modules:
  0.0 292.4 jit_solution(17640571249118401597)
XLA Ops:
  0.6 2.2 make_table.1
  2.8 11.2 %all-to-all-start = ((f32[128,1,128]{2,1,0:T(1,128)}), f32[128,1,128]{2,1,0:T(1,128)S(1)}, u32[]{:S(2)}, u32[]{:S(2)}) async-start(f32[128,1,128]{2,1,0:T(1,128)} %bitcast.18), calls=%async_computation | async-start | bytes 131072 | tf_op jit(solution)/shard_map/all_to_all | solution.py:520
  14.0 7.1 %unit_vectors.1 = (bf16[2048,1024]{1,0:T(8,128)(2,1)}, bf16[2048,1024]{1,0:T(8,128)(2,1)}) custom-call(bf16[2048,1024]{1,0:T(8,128)(2,1)} %lists_ref.1, bf16[2048,1024]{1,0:T(8,128)(2,1)} %groups_ref.1), custom_call_target="tpu_custom_call" | custom-call | flops 16777216 | bytes 16777216 | tf_op jit(solution)/shard_map/unit_vectors/pallas_call | solution.py:115
  21.1 2.2 all-to-all-done
  23.3 0.6 copy-done.5
  24.0 5.0 %pick_lists.1 = (bf16[32,128,1024]{2,1,0:T(8,128)(2,1)S(1)}, s32[32]{0:T(128)}, f32[2,16,32,128]{3,2,1,0:T(8,128)S(1)}, f32[8,128]{1,0:T(8,128)S(1)}) custom-call(f32[16,8,128]{2,1,0:T(8,128)} %bitcast.19, f32[128,128]{1,0:T(8,128)} %get-tuple-element.15.table_ref, bf16[16,128,1024]{2,1,0:T(8,128)(2,1)} %bitcast.17), custom_call_target="tpu_custom_call" | custom-call | tf_op jit(solution)/shard_map/pick_lists/pallas_call | solution.py:186
  29.0 0.0 copy-start
  29.0 0.0 copy-start.1
  29.0 0.0 copy-start.2
  29.0 0.0 copy-start.3
  29.1 100.6 %all_to_all.30 = bf16[16,256,1024]{2,1,0:T(8,128)(2,1)S(1)} all-to-all(bf16[16,256,1024]{2,1,0:T(8,128)(2,1)S(1)} %bitcast.14), channel_id=1, replica_groups=mesh['rows'=16,'cents'=8] {'rows'}, dimensions={0} | all-to-all | bytes 16777216 | tf_op jit(solution)/shard_map/all_to_all | solution.py:514
  129.6 0.0 copy-done
  129.6 0.0 copy-done.1
  129.6 0.0 copy-done.2
  129.7 0.0 copy-done.3
  129.7 7.1 %scores.1 = (f32[8,8,256,128]{3,2,1,0:T(8,128)S(1)}, f32[16,32,128]{2,1,0:T(8,128)S(1)}, f32[8,256,128]{2,1,0:T(8,128)S(1)}) custom-call(s32[64]{0:T(128)S(1)} %copy-done.2, s32[8]{0:T(128)S(1)} %copy-done.3, bf16[8,256,1024]{2,1,0:T(8,128)(2,1)S(1)} %bitcast.12, f32[16,128]{1,0:T(8,128)S(1)} %bitcast.16, bf16[32,128,1024]{2,1,0:T(8,128)(2,1)S(1)} %bitcast.11), custom_call_target="tpu_custom_call" | custom-call | tf_op jit(solution)/shard_map/scores/pallas_call | solution.py:263
  136.7 11.6 %all_to_all.31.got_ref = f32[16,32,128]{2,1,0:T(8,128)S(1)} all-to-all(f32[16,32,128]{2,1,0:T(8,128)S(1)} %get-tuple-element.23), channel_id=1, replica_groups=mesh['rows'=16,'cents'=8] {'rows'}, dimensions={0} | all-to-all | bytes 524288 | tf_op jit(solution)/shard_map/all_to_all | solution.py:514
  148.4 2.3 turn.2
  150.7 11.6 %all_to_all.32.got_ref = f32[16,32,128]{2,1,0:T(8,128)S(1)} all-to-all(f32[16,32,128]{2,1,0:T(8,128)S(1)} %turn.2), channel_id=1, replica_groups=mesh['rows'=16,'cents'=8] {'rows'}, dimensions={0} | all-to-all | bytes 524288 | tf_op jit(solution)/shard_map/all_to_all | solution.py:514
  162.3 2.3 turn.3
  164.6 11.6 %all_to_all.33.got_ref = f32[16,32,128]{2,1,0:T(8,128)S(1)} all-to-all(f32[16,32,128]{2,1,0:T(8,128)S(1)} %turn.3), channel_id=1, replica_groups=mesh['rows'=16,'cents'=8] {'rows'}, dimensions={0} | all-to-all | bytes 524288 | tf_op jit(solution)/shard_map/all_to_all | solution.py:514
  176.2 11.9 %final_pass.1 = bf16[16,2064,128]{2,1,0:T(8,128)(2,1)S(1)} custom-call(s32[64]{0:T(128)S(1)} %copy-done.2, f32[8,8,256,128]{3,2,1,0:T(8,128)S(1)} %get-tuple-element.21.kernel_ref, f32[8,256,128]{2,1,0:T(8,128)S(1)} %get-tuple-element.22.weight_ref, bf16[8,256,1024]{2,1,0:T(8,128)(2,1)S(1)} %bitcast.13, f32[16,32,128]{2,1,0:T(8,128)S(1)} %all_to_all.33.got_ref, ...), custom_call_target="tpu_custom_call" | custom-call | tf_op jit(solution)/shard_map/final_pass/pallas_call | solution.py:409
  188.1 96.9 %all_to_all.34.got_ref = bf16[16,2064,128]{2,1,0:T(8,128)(2,1)S(1)} all-to-all(bf16[16,2064,128]{2,1,0:T(8,128)(2,1)S(1)} %final_pass.1), channel_id=1, replica_groups=mesh['rows'=16,'cents'=8] {'rows'}, dimensions={0} | all-to-all | bytes 16908288 | tf_op jit(solution)/shard_map/all_to_all | solution.py:514
  285.1 7.4 %merge.1 = (f32[16,128,1024]{2,1,0:T(8,128)}, f32[16,128]{1,0:T(8,128)}) custom-call(s32[32]{0:T(128)S(1)} %copy-done.4, bf16[16,2064,128]{2,1,0:T(8,128)(2,1)S(1)} %all_to_all.34.got_ref, f32[8,128]{1,0:T(8,128)S(1)} %get-tuple-element.25.target_ref), custom_call_target="tpu_custom_call" | custom-call | tf_op jit(solution)/shard_map/merge/pallas_call | solution.py:494
  (3 shorter events, 0.0 us)
Async XLA Ops:
  2.8 20.5 %all-to-all-start = ((f32[128,1,128]{2,1,0:T(1,128)}), f32[128,1,128]{2,1,0:T(1,128)S(1)}, u32[]{:S(2)}, u32[]{:S(2)}) async-start(f32[128,1,128]{2,1,0:T(1,128)} %bitcast.18), calls=%async_computation | async-start | bytes 131072 | tf_op jit(solution)/shard_map/all_to_all | solution.py:520
  23.3 0.6 copy-start.5
  29.0 100.6 %copy-start = (bf16[2048,1024]{1,0:T(8,128)(2,1)S(1)}, bf16[2048,1024]{1,0:T(8,128)(2,1)}, u32[]{:S(2)}) copy-start(bf16[2048,1024]{1,0:T(8,128)(2,1)} %get-tuple-element.19) | copy-start | bytes 12582916
  29.0 100.6 %copy-start.1 = (f32[2048]{0:T(1024)S(1)}, f32[2048]{0:T(1024)}, u32[]{:S(2)}) copy-start(f32[2048]{0:T(1024)} %param.7) | copy-start | bytes 24580
  29.0 100.6 %copy-start.2 = (s32[64]{0:T(128)S(1)}, s32[64]{0:T(128)}, u32[]{:S(2)}) copy-start(s32[64]{0:T(128)} %get-tuple-element.18.dist_ref) | copy-start | bytes 772
  29.0 100.6 %copy-start.3 = (s32[8]{0:T(128)S(1)}, s32[8]{0:T(128)}, u32[]{:S(2)}) copy-start(s32[8]{0:T(128)} %count_ref.1) | copy-start | bytes 100
  188.1 96.9 %copy-start.4 = (s32[32]{0:T(128)S(1)}, s32[32]{0:T(128)}, u32[]{:S(2)}) copy-start(s32[32]{0:T(128)} %get-tuple-element.17.wanted_ref) | copy-start | bytes 388

commit v4 on v3

--- a/solution.py
+++ b/solution.py
@@ -20,6 +20,7 @@
 K_TOTAL = DEVICES * CBD * CB
 ROWS_X = USE * CB * (D // 128)
 ROWS_P = ROWS_X + 16
+HOLDER_BITS = (CBD * NC).bit_length() - 1
 
 BETA = 32.0
 EPSILON = 1e-06
@@ -36,23 +37,35 @@
     return (widened * lax.rsqrt(mean + EPSILON)).astype(BF16)
 
 
-def table_kernel(ids_ref, weight_ref, table_ref, dist_ref, low_ref, high_ref):
+def table_kernel(
+    ids_ref, weight_ref, lists_ref, table_ref, dist_ref, unit_ref, low_ref, high_ref, raw, sem
+):
+    def load(n):
+        return pltpu.make_async_copy(lists_ref.at[n], raw.at[n], sem.at[n])
+
+    for n in range(CBD):
+        load(n).start()
     for o in range(NR):
         low_ref[o] = -1
         high_ref[o] = -1
-
-    @pl.loop(0, NBD)
-    def _(b):
-        for k in range(MAXC):
+    part = MAXC // 2
+
+    @pl.loop(0, CBD)
+    def _(n):
+        load(n).wait()
+        for m in range(part):
+            b = n >> 1
+            k = (n & 1) * part + m
             number = ids_ref[b, k]
-            holder = number // (CBD * NC)
-            local = number % CBD
+            holder = number >> HOLDER_BITS
+            local = number & (CBD - 1)
             seen = low_ref[holder]
             low = jnp.where(seen < 0, local, seen)
             low_ref[holder] = low
             rank = jnp.where(local != low, 1, 0)
             high_ref[holder] = jnp.where(rank == 1, local, high_ref[holder])
-            dist_ref[b * MAXC + k] = holder * USE + rank
+            dist_ref[n * part + m] = holder * USE + rank
+        unit_ref[n] = unit_rows(raw[n])
 
     weight = jnp.sum(jnp.sum(weight_ref[...], axis=0, keepdims=True), axis=1, keepdims=True)
     lane = lax.broadcasted_iota(jnp.int32, (1, CB), 1)
@@ -67,65 +80,26 @@
     table_ref[...] = jnp.broadcast_to(row, (DEVICES, CB))
 
 
-def make_table(block_ids, weight_rows):
+def make_table(block_ids, weight_rows, centroids):
+    smem = pl.BlockSpec(memory_space=pltpu.SMEM)
     return pl.pallas_call(
         table_kernel,
-        in_specs=[pl.BlockSpec(memory_space=pltpu.SMEM), HELD],
-        out_specs=[HELD, pl.BlockSpec(memory_space=pltpu.SMEM)],
+        in_specs=[smem, HELD, pl.BlockSpec(memory_space=pl.ANY)],
+        out_specs=[HELD, smem, HELD],
         out_shape=[
-            jax.ShapeDtypeStruct((DEVICES, CB), F32),
+            pltpu.VMEM((DEVICES, CB), F32),
             jax.ShapeDtypeStruct((NBD * MAXC,), jnp.int32),
-        ],
-        scratch_shapes=[pltpu.SMEM((NR,), jnp.int32), pltpu.SMEM((NR,), jnp.int32)],
+            pltpu.VMEM((CBD, CB, D), BF16),
+        ],
+        scratch_shapes=[
+            pltpu.SMEM((NR,), jnp.int32),
+            pltpu.SMEM((NR,), jnp.int32),
+            pltpu.VMEM((CBD, CB, D), BF16),
+            pltpu.SemaphoreType.DMA((CBD,)),
+        ],
+        compiler_params=pltpu.CompilerParams(vmem_limit_bytes=57 << 20),
         name="make_table",
-    )(block_ids, weight_rows)
-
-
-def unit_kernel(lists_ref, groups_ref, unit_ref, rows_ref, raw, made, in_sem, out_sem):
-    def span(n):
-        return pl.ds(pl.multiple_of(n * CB, CB), CB)
-
-    def load(source, n, at):
-        return pltpu.make_async_copy(source.at[span(n)], raw.at[at], in_sem.at[at])
-
-    def store(target, n, at):
-        return pltpu.make_async_copy(made.at[at], target.at[span(n)], out_sem.at[at])
-
-    pairs = ((lists_ref, unit_ref, 0), (groups_ref, rows_ref, CBD))
-    for source, _, base in pairs:
-        for n in range(CBD):
-            load(source, n, base + n).start()
-    for source, target, base in pairs:
-
-        @pl.loop(0, CBD)
-        def _(n, source=source, target=target, base=base):
-            load(source, n, base + n).wait()
-            made[base + n] = unit_rows(raw[base + n])
-            store(target, n, base + n).start()
-
-    for _, target, base in pairs:
-
-        @pl.loop(0, CBD)
-        def _(n, target=target, base=base):
-            store(target, n, base + n).wait()
-
-
-def unit_vectors(centroids, groups):
-    far = pl.BlockSpec(memory_space=pl.ANY)
-    return pl.pallas_call(
-        unit_kernel,
-        in_specs=[far, far],
-        out_specs=[far, far],
-        out_shape=[jax.ShapeDtypeStruct(centroids.shape, BF16), jax.ShapeDtypeStruct(groups.shape, BF16)],
-        scratch_shapes=[
-            pltpu.VMEM((2 * CBD, CB, D), BF16),
-            pltpu.VMEM((2 * CBD, CB, D), BF16),
-            pltpu.SemaphoreType.DMA((2 * CBD,)),
-            pltpu.SemaphoreType.DMA((2 * CBD,)),
-        ],
-        cost_estimate=pl.CostEstimate(flops=1 << 24, bytes_accessed=1 << 24, transcendentals=1 << 12),
-        name="unit_vectors",
-    )(centroids, groups)
+    )(block_ids, weight_rows, centroids)
 
 
 def prepare(rows, mine, tables_ref, same_ref, target_ref):
@@ -153,39 +127,31 @@
     target_ref,
     numbers,
     scalars,
-    unit,
-    in_sem,
     move_sem,
 ):
     me = lax.axis_index("rows")
     side = lax.axis_index("cents")
 
-    def load(j):
-        return pltpu.make_async_copy(lists_ref.at[j], unit.at[j], in_sem.at[j])
-
-    for j in range(CBD):
-        load(j).start()
     rows = jnp.concatenate([tables_ref[r, pl.ds(side, 1), :] for r in range(NR)], axis=0)
     numbers[...] = rows.astype(jnp.int32)
     move = pltpu.make_async_copy(numbers, scalars, move_sem)
     move.start()
     prepare(rows, table_ref[:1], tables_ref, same_ref, target_ref)
+
     move.wait()
-    for j in range(CBD):
-        load(j).wait()
 
     @pl.loop(0, NR)
     def _(r):
         for u in range(USE):
             j = scalars[r, me * USE + u]
             wanted_ref[r * USE + u] = j
-            out_ref[r * USE + u] = unit[j]
+            out_ref[r * USE + u] = lists_ref[j]
 
 
 def pick_lists(tables, table, unit):
     return pl.pallas_call(
         pick_kernel,
-        in_specs=[HELD, HELD, pl.BlockSpec(memory_space=pl.ANY)],
+        in_specs=[HELD, HELD, HELD],
         out_specs=[HELD, pl.BlockSpec(memory_space=pltpu.SMEM), HELD, HELD],
         out_shape=[
             pltpu.VMEM((ND, CB, D), BF16),
@@ -196,11 +162,9 @@
         scratch_shapes=[
             pltpu.VMEM((NR, CB), jnp.int32),
             pltpu.SMEM((NR, CB), jnp.int32),
-            pltpu.VMEM((CBD, CB, D), BF16),
-            pltpu.SemaphoreType.DMA((CBD,)),
             pltpu.SemaphoreType.DMA,
         ],
-        compiler_params=pltpu.CompilerParams(vmem_limit_bytes=54 << 20),
+        compiler_params=LIMIT,
         name="pick_lists",
     )(tables, table, unit)
 
@@ -222,7 +186,7 @@
 
 
 def scores_kernel(dist_ref, count_ref, *refs):
-    rows_ref, mass_ref, lists_ref, kernel_ref, out_ref, weight_ref, parts_ref = refs
+    groups_ref, mass_ref, lists_ref, kernel_ref, out_ref, rows_ref, weight_ref, parts_ref = refs
     step = pl.program_id(0)
 
     @pl.when(step == 0)
@@ -232,7 +196,8 @@
     for n in range(STEP):
         b = step * STEP + n
         count = count_ref[b]
-        rows = rows_ref[b]
+        rows = unit_rows(groups_ref[b])
+        rows_ref[b] = rows
         halves = []
         for h in range(RB // CB):
             flat = jnp.broadcast_to(mass_ref[pl.ds(b * (RB // CB) + h, 1), :], (CB, CB))
@@ -259,24 +224,25 @@
         spread(parts_ref, out_ref)
 
 
-def first_pass(dist, counts, rows, weight_rows, lists):
+def first_pass(dist, counts, groups, weight_rows, lists):
     return pl.pallas_call(
         scores_kernel,
         grid_spec=pltpu.PrefetchScalarGridSpec(
             num_scalar_prefetch=2,
             grid=(NBD // STEP,),
             in_specs=[HELD] * 3,
-            out_specs=[HELD] * 3,
+            out_specs=[HELD] * 4,
             scratch_shapes=[pltpu.VMEM((ND, CB), F32)],
         ),
         out_shape=[
             pltpu.VMEM((NBD, MAXC, RB, CB), F32),
             jax.ShapeDtypeStruct((NR, ND, CB), F32),
+            pltpu.VMEM((NBD, RB, D), BF16),
             pltpu.VMEM((NBD, RB, CB), F32),
         ],
         compiler_params=LIMIT,
         name="scores",
-    )(dist, counts, rows, weight_rows, lists)
+    )(dist, counts, groups, weight_rows, lists)
 
 
 def new_scales(got_ref, same_ref, target_ref, scales_ref):
@@ -371,7 +337,7 @@
             plan_keep[b * MAXC + k] = jnp.transpose(plan.astype(BF16))
             n = seen_ref[d]
             seen_ref[d] = n + 1
-            order_ref[d // 2 * 4 + jnp.where(d % 2 == 0, n, 3 - n)] = b * MAXC + k
+            order_ref[(d >> 1) * 4 + jnp.where(d & 1 == 0, n, 3 - n)] = b * MAXC + k
 
     @pl.when(step >= NBD)
     def _():
@@ -382,7 +348,7 @@
 
         def emit(u, chosen):
             left = jnp.concatenate([plans[n] for n in chosen], axis=1)
-            right = jnp.concatenate([rows_ref[slots[n] // MAXC] for n in chosen], axis=0)
+            right = jnp.concatenate([rows_ref[slots[n] >> 3] for n in chosen], axis=0)
             total = jnp.dot(left, right, preferred_element_type=F32)
             for c in range(D // 128):
                 at = c * USE * CB + u * CB
@@ -428,7 +394,7 @@
 
 
 def merge_kernel(
-    wanted_ref, got_ref, target_ref, out_ref, load_ref, held, order_ref, start_ref, out_sem
+    wanted_ref, got_ref, target_ref, out_ref, load_ref, held, from_ref, into_ref, start_ref, out_sem
 ):
     chunks = D // 128
 
@@ -460,20 +426,24 @@
         j = wanted_ref[i]
         at = start_ref[j]
         start_ref[j] = at + 1
-        order_ref[at] = i
+        from_ref[at] = i
+        into_ref[at] = j
 
     @pl.loop(0, chunks)
     def _(s):
-        total = jnp.zeros((CB, 128), F32)
-        last = -1
-        for n in range(ND):
-            i = order_ref[n]
-            j = wanted_ref[i]
-            at = pl.multiple_of(s * (USE * CB) + (i % USE) * CB, CB)
-            part = got_ref[i // USE, pl.ds(at, CB), :].astype(F32)
-            total = part + jnp.where(j == last, total, 0.0)
-            held[s, j] = total
-            last = j
+        def add(group, carry):
+            total, last = carry
+            for m in range(4):
+                i = from_ref[group * 4 + m]
+                j = into_ref[group * 4 + m]
+                at = pl.multiple_of(s * (USE * CB) + (i & 1) * CB, CB)
+                part = got_ref[i >> 1, pl.ds(at, CB), :].astype(F32)
+                total = part + jnp.where(j == last, total, 0.0)
+                held[s, j] = total
+                last = j
+            return total, last
+
+        lax.fori_loop(0, ND // 4, add, (jnp.zeros((CB, 128), F32), jnp.int32(-1)))
         put(s).start()
 
     load_ref[...] = jnp.zeros_like(load_ref)
@@ -498,6 +468,7 @@
         scratch_shapes=[
             pltpu.VMEM((chunks, CBD, CB, 128), F32),
             pltpu.SMEM((ND,), jnp.int32),
+            pltpu.SMEM((ND,), jnp.int32),
             pltpu.SMEM((CBD + 2,), jnp.int32),
             pltpu.SemaphoreType.DMA((chunks,)),
         ],
@@ -516,18 +487,17 @@
 
 def body(groups, centroids, row_weight, block_ids, block_counts):
     weight_rows = row_weight.reshape(NBD * RB // CB, CB)
-    table, dist = make_table(block_ids, weight_rows)
+    table, dist, unit = make_table(block_ids, weight_rows, centroids.reshape(CBD, CB, D))
     tables = lax.all_to_all(
         table.reshape(DEVICES, 1, CB), ("rows", "cents"), split_axis=0, concat_axis=0, tiled=True
     ).reshape(NR, NC, CB)
-    unit, rows = unit_vectors(centroids, groups)
     picked, wanted, same, target = pick_lists(
-        tables, table, unit.reshape(CBD, CB, D)
+        tables, table, unit
     )
-    rows = rows.reshape(NBD, RB, D)
+    groups = groups.reshape(NBD, RB, D)
     lists = exchange(picked.reshape(NR, USE * CB, D)).reshape(ND, CB, D)
 
-    kernel, parts, weights = first_pass(dist, block_counts, rows, weight_rows, lists)
+    kernel, parts, rows, weights = first_pass(dist, block_counts, groups, weight_rows, lists)
     got = exchange(parts)
     for _ in range(ITERS - 1):
         got = exchange(turn(dist, kernel, weights, got, same, target))

time: 293 us -> 291 us (level)
  blocking collectives: 232 us -> 251 us
  starting transfers between devices: 11.2 us -> 0 us
  Pallas kernels: 45.3 us -> 37.2 us
    all_to_all x0 -> x1, blocking collectives: none -> 20.3 us  [body(): lax.all_to_all(table.reshape(DEVICES, 1, CB), ('rows', 'cents'), split_ax...]
    all_to_all x1 -> x0, starting transfers between devices: 11.2 us -> none  [body(): lax.all_to_all(table.reshape(DEVICES, 1, CB), ('rows', 'cents'), split_ax...]
    pallas_call x3 -> x2, Pallas kernels: 14.3 us -> 7.34 us  [the longest x1 4.49 us: make_table(): pl.pallas_call(table_kernel, in_specs=[smem, HELD, pl.BlockSpec(memory_sp...]
  transfers between devices with their start and end apart: 1 -> 0, of which waited for: 1 -> 0; matrix products, arithmetic and copies ran while one was open for 0% -> 0% of each run, Pallas kernels for 2% -> 0%
where the time goes in v4:
time: 291 us; the launch traced here: 289 us
  blocking collectives  251 us (86%)
  Pallas kernels  37.2 us (13%)
    all_to_all x5, blocking collectives, exchange(): lax.all_to_all(values, 'rows', split_axis=0, concat_axis=0, tiled=True)  231 us
    all_to_all x1, blocking collectives, body(): lax.all_to_all(table.reshape(DEVICES, 1, CB), ('rows', 'cents'), split_ax...  20.3 us
    pallas_call x1, Pallas kernels, final_pass(): pl.pallas_call(final_kernel, grid_spec=pltpu.PrefetchScalarGridSpec(num_s...  11.6 us
    pallas_call x1, Pallas kernels, first_pass(): pl.pallas_call(scores_kernel, grid_spec=pltpu.PrefetchScalarGridSpec(num_...  7.6 us
    pallas_call x1, Pallas kernels, merge(): pl.pallas_call(merge_kernel, in_specs=[pl.BlockSpec(memory_space=pltpu.SM...  6.06 us

profile of v4, /device:TPU:0, one launch (start us, length us, event | category | flops | bytes accessed | tf_op | source)
XLA Modules:
  0.0 288.9 jit_solution(1949437241728740657)
XLA Ops:
  0.6 4.5 %make_table.1 = (f32[128,128]{1,0:T(8,128)S(1)}, s32[64]{0:T(128)}, bf16[16,128,1024]{2,1,0:T(8,128)(2,1)S(1)}) custom-call(s32[8,8]{1,0:T(8,128)} %ids_ref.1, f32[16,128]{1,0:T(8,128)} %bitcast.16, bf16[16,128,1024]{2,1,0:T(8,128)(2,1)} %bitcast.18), custom_call_target="tpu_custom_call" | custom-call | tf_op jit(solution)/shard_map/make_table/pallas_call | solution.py:85
  5.1 20.3 %all_to_all.30 = f32[128,1,128]{2,1,0:T(1,128)S(1)} all-to-all(f32[128,1,128]{2,1,0:T(1,128)S(1)} %bitcast.14), channel_id=1, replica_groups=mesh['rows'=16,'cents'=8] {'rows','cents'}, dimensions={0} | all-to-all | bytes 131072 | tf_op jit(solution)/shard_map/all_to_all | solution.py:491
  25.4 2.9 pick_lists.1
  28.3 0.0 copy-start
  28.3 0.0 copy-start.1
  28.3 0.0 copy-start.2
  28.3 0.0 copy-start.3
  28.4 98.9 %all_to_all.31 = bf16[16,256,1024]{2,1,0:T(8,128)(2,1)S(1)} all-to-all(bf16[16,256,1024]{2,1,0:T(8,128)(2,1)S(1)} %bitcast.12), channel_id=1, replica_groups=mesh['rows'=16,'cents'=8] {'rows'}, dimensions={0} | all-to-all | bytes 16777216 | tf_op jit(solution)/shard_map/all_to_all | solution.py:485
  127.3 0.0 copy-done
  127.3 0.0 copy-done.1
  127.3 0.0 copy-done.2
  127.3 0.0 copy-done.3
  127.3 7.6 %scores.1 = (f32[8,8,256,128]{3,2,1,0:T(8,128)S(1)}, f32[16,32,128]{2,1,0:T(8,128)S(1)}, bf16[8,256,1024]{2,1,0:T(8,128)(2,1)S(1)}, f32[8,256,128]{2,1,0:T(8,128)S(1)}) custom-call(s32[64]{0:T(128)S(1)} %copy-done.2, s32[8]{0:T(128)S(1)} %copy-done.3, bf16[8,256,1024]{2,1,0:T(8,128)(2,1)S(1)} %bitcast.13, f32[16,128]{1,0:T(8,128)S(1)} %bitcast.17, ...), custom_call_target="tpu_custom_call" | custom-call | tf_op jit(solution)/shard_map/scores/pallas_call | solution.py:228
  134.9 11.6 %all_to_all.32.got_ref = f32[16,32,128]{2,1,0:T(8,128)S(1)} all-to-all(f32[16,32,128]{2,1,0:T(8,128)S(1)} %get-tuple-element.23), channel_id=1, replica_groups=mesh['rows'=16,'cents'=8] {'rows'}, dimensions={0} | all-to-all | bytes 524288 | tf_op jit(solution)/shard_map/all_to_all | solution.py:485
  146.6 2.3 turn.2
  148.9 11.6 %all_to_all.33.got_ref = f32[16,32,128]{2,1,0:T(8,128)S(1)} all-to-all(f32[16,32,128]{2,1,0:T(8,128)S(1)} %turn.2), channel_id=1, replica_groups=mesh['rows'=16,'cents'=8] {'rows'}, dimensions={0} | all-to-all | bytes 524288 | tf_op jit(solution)/shard_map/all_to_all | solution.py:485
  160.5 2.3 turn.3
  162.8 11.6 %all_to_all.34.got_ref = f32[16,32,128]{2,1,0:T(8,128)S(1)} all-to-all(f32[16,32,128]{2,1,0:T(8,128)S(1)} %turn.3), channel_id=1, replica_groups=mesh['rows'=16,'cents'=8] {'rows'}, dimensions={0} | all-to-all | bytes 524288 | tf_op jit(solution)/shard_map/all_to_all | solution.py:485
  174.4 11.6 %final_pass.1 = bf16[16,2064,128]{2,1,0:T(8,128)(2,1)S(1)} custom-call(s32[64]{0:T(128)S(1)} %copy-done.2, f32[8,8,256,128]{3,2,1,0:T(8,128)S(1)} %get-tuple-element.20.kernel_ref, f32[8,256,128]{2,1,0:T(8,128)S(1)} %get-tuple-element.21.weight_ref, bf16[8,256,1024]{2,1,0:T(8,128)(2,1)S(1)} %get-tuple-element.22.rows_ref, ...), custom_call_target="tpu_custom_call" | custom-call | tf_op jit(solution)/shard_map/final_pass/pallas_call | solution.py:375
  186.0 96.9 %all_to_all.35.got_ref = bf16[16,2064,128]{2,1,0:T(8,128)(2,1)S(1)} all-to-all(bf16[16,2064,128]{2,1,0:T(8,128)(2,1)S(1)} %final_pass.1), channel_id=1, replica_groups=mesh['rows'=16,'cents'=8] {'rows'}, dimensions={0} | all-to-all | bytes 16908288 | tf_op jit(solution)/shard_map/all_to_all | solution.py:485
  282.8 6.1 %merge.1 = (f32[16,128,1024]{2,1,0:T(8,128)}, f32[16,128]{1,0:T(8,128)}) custom-call(s32[32]{0:T(128)S(1)} %get-tuple-element.17.wanted_ref, bf16[16,2064,128]{2,1,0:T(8,128)(2,1)S(1)} %all_to_all.35.got_ref, f32[8,128]{1,0:T(8,128)S(1)} %get-tuple-element.25.target_ref), custom_call_target="tpu_custom_call" | custom-call | tf_op jit(solution)/shard_map/merge/pallas_call | solution.py:464
Async XLA Ops:
  28.3 99.0 %copy-start = (bf16[2048,1024]{1,0:T(8,128)(2,1)S(1)}, bf16[2048,1024]{1,0:T(8,128)(2,1)}, u32[]{:S(2)}) copy-start(bf16[2048,1024]{1,0:T(8,128)(2,1)} %param.5) | copy-start | bytes 12582916
  28.3 99.0 %copy-start.1 = (f32[2048]{0:T(1024)S(1)}, f32[2048]{0:T(1024)}, u32[]{:S(2)}) copy-start(f32[2048]{0:T(1024)} %param.7) | copy-start | bytes 24580
  28.3 99.0 %copy-start.2 = (s32[64]{0:T(128)S(1)}, s32[64]{0:T(128)}, u32[]{:S(2)}) copy-start(s32[64]{0:T(128)} %get-tuple-element.18.dist_ref) | copy-start | bytes 772
  28.3 99.0 %copy-start.3 = (s32[8]{0:T(128)S(1)}, s32[8]{0:T(128)}, u32[]{:S(2)}) copy-start(s32[8]{0:T(128)} %count_ref.1) | copy-start | bytes 100

commit v5 on v4

--- a/solution.py
+++ b/solution.py
@@ -20,6 +20,7 @@
 K_TOTAL = DEVICES * CBD * CB
 ROWS_X = USE * CB * (D // 128)
 ROWS_P = ROWS_X + 16
+EARLY = NBD // 2
 HOLDER_BITS = (CBD * NC).bit_length() - 1
 
 BETA = 32.0
@@ -182,7 +183,7 @@
         out_ref[r] = parts
 
 
-STEP = 2
+STEP = 4
 
 
 def scores_kernel(dist_ref, count_ref, *refs):
@@ -270,17 +271,19 @@
 def turn_kernel(
     dist_ref, kernel_ref, weight_ref, got_ref, same_ref, target_ref, out_ref, scales_ref, parts_ref
 ):
-    b = pl.program_id(0)
-
-    @pl.when(b == 0)
+    step = pl.program_id(0)
+
+    @pl.when(step == 0)
     def _():
         new_scales(got_ref, same_ref, target_ref, scales_ref)
         parts_ref[...] = jnp.zeros_like(parts_ref)
 
-    row_scale = row_pass(kernel_ref, weight_ref, scales_ref, dist_ref, b)
-    column_pass(kernel_ref, row_scale, dist_ref, b, parts_ref)
-
-    @pl.when(b == NBD - 1)
+    for n in range(STEP):
+        b = step * STEP + n
+        row_scale = row_pass(kernel_ref, weight_ref, scales_ref, dist_ref, b)
+        column_pass(kernel_ref, row_scale, dist_ref, b, parts_ref)
+
+    @pl.when(step == NBD // STEP - 1)
     def _():
         spread(parts_ref, out_ref)
 
@@ -290,7 +293,7 @@
         turn_kernel,
         grid_spec=pltpu.PrefetchScalarGridSpec(
             num_scalar_prefetch=1,
-            grid=(NBD,),
+            grid=(NBD // STEP,),
             in_specs=[HELD] * 5,
             out_specs=HELD,
             scratch_shapes=[pltpu.VMEM((ND, CB), F32), pltpu.VMEM((ND, CB), F32)],
@@ -326,22 +329,23 @@
         for d in range(ND):
             seen_ref[d] = 0
 
-    @pl.when(step < NBD)
-    def _():
-        b = step
-        row_scale = row_pass(kernel_ref, weight_ref, scales_ref, dist_ref, b)
-        for k in range(MAXC):
-            d = dist_ref[b * MAXC + k]
-            plan = row_scale * kernel_ref[b, k] * scales_ref[pl.ds(d, 1), :]
-            parts_ref[pl.ds(d, 1), :] += jnp.sum(plan, axis=0, keepdims=True)
-            plan_keep[b * MAXC + k] = jnp.transpose(plan.astype(BF16))
-            n = seen_ref[d]
-            seen_ref[d] = n + 1
-            order_ref[(d >> 1) * 4 + jnp.where(d & 1 == 0, n, 3 - n)] = b * MAXC + k
-
-    @pl.when(step >= NBD)
-    def _():
-        holder = step - NBD
+    @pl.when(step < EARLY)
+    def _():
+        for half in range(NBD // EARLY):
+            b = step * (NBD // EARLY) + half
+            row_scale = row_pass(kernel_ref, weight_ref, scales_ref, dist_ref, b)
+            for k in range(MAXC):
+                d = dist_ref[b * MAXC + k]
+                plan = row_scale * kernel_ref[b, k] * scales_ref[pl.ds(d, 1), :]
+                parts_ref[pl.ds(d, 1), :] += jnp.sum(plan, axis=0, keepdims=True)
+                plan_keep[b * MAXC + k] = jnp.transpose(plan.astype(BF16))
+                n = seen_ref[d]
+                seen_ref[d] = n + 1
+                order_ref[(d >> 1) * 4 + jnp.where(d & 1 == 0, n, 3 - n)] = b * MAXC + k
+
+    @pl.when(step >= EARLY)
+    def _():
+        holder = step - EARLY
         slots = [order_ref[holder * 4 + n] for n in range(4)]
         plans = [plan_keep[p] for p in slots]
         first = seen_ref[holder * 2]
@@ -376,7 +380,7 @@
         final_kernel,
         grid_spec=pltpu.PrefetchScalarGridSpec(
             num_scalar_prefetch=1,
-            grid=(NBD + NR,),
+            grid=(EARLY + NR,),
             in_specs=[HELD] * 6,
             out_specs=HELD,
             scratch_shapes=[

time: 291 us -> 288 us (0.990)
  no operation moved by 1% of the time
where the time goes in v5:
time: 288 us; the launch traced here: 287 us
  blocking collectives  251 us (87%)
  Pallas kernels  35.4 us (12%)
    all_to_all x5, blocking collectives, exchange(): lax.all_to_all(values, 'rows', split_axis=0, concat_axis=0, tiled=True)  231 us
    all_to_all x1, blocking collectives, body(): lax.all_to_all(table.reshape(DEVICES, 1, CB), ('rows', 'cents'), split_ax...  20.3 us
    pallas_call x1, Pallas kernels, final_pass(): pl.pallas_call(final_kernel, grid_spec=pltpu.PrefetchScalarGridSpec(num_s...  11 us
    pallas_call x1, Pallas kernels, first_pass(): pl.pallas_call(scores_kernel, grid_spec=pltpu.PrefetchScalarGridSpec(num_...  7.1 us
    pallas_call x1, Pallas kernels, merge(): pl.pallas_call(merge_kernel, in_specs=[pl.BlockSpec(memory_space=pltpu.SM...  6.09 us

profile of v5, /device:TPU:0, one launch (start us, length us, event | category | flops | bytes accessed | tf_op | source)
XLA Modules:
  0.0 287.1 jit_solution(12621437536100219868)
XLA Ops:
  0.6 4.5 %make_table.1 = (f32[128,128]{1,0:T(8,128)S(1)}, s32[64]{0:T(128)}, bf16[16,128,1024]{2,1,0:T(8,128)(2,1)S(1)}) custom-call(s32[8,8]{1,0:T(8,128)} %ids_ref.1, f32[16,128]{1,0:T(8,128)} %bitcast.16, bf16[16,128,1024]{2,1,0:T(8,128)(2,1)} %bitcast.18), custom_call_target="tpu_custom_call" | custom-call | tf_op jit(solution)/shard_map/make_table/pallas_call | solution.py:86
  5.1 20.3 %all_to_all.30 = f32[128,1,128]{2,1,0:T(1,128)S(1)} all-to-all(f32[128,1,128]{2,1,0:T(1,128)S(1)} %bitcast.14), channel_id=1, replica_groups=mesh['rows'=16,'cents'=8] {'rows','cents'}, dimensions={0} | all-to-all | bytes 131072 | tf_op jit(solution)/shard_map/all_to_all | solution.py:495
  25.4 2.9 pick_lists.1
  28.3 0.0 copy-start
  28.3 0.0 copy-start.1
  28.3 0.0 copy-start.2
  28.3 0.0 copy-start.3
  28.4 98.9 %all_to_all.31 = bf16[16,256,1024]{2,1,0:T(8,128)(2,1)S(1)} all-to-all(bf16[16,256,1024]{2,1,0:T(8,128)(2,1)S(1)} %bitcast.12), channel_id=1, replica_groups=mesh['rows'=16,'cents'=8] {'rows'}, dimensions={0} | all-to-all | bytes 16777216 | tf_op jit(solution)/shard_map/all_to_all | solution.py:489
  127.3 0.0 copy-done
  127.3 0.0 copy-done.1
  127.3 0.0 copy-done.2
  127.3 0.0 copy-done.3
  127.3 7.1 %scores.1 = (f32[8,8,256,128]{3,2,1,0:T(8,128)S(1)}, f32[16,32,128]{2,1,0:T(8,128)S(1)}, bf16[8,256,1024]{2,1,0:T(8,128)(2,1)S(1)}, f32[8,256,128]{2,1,0:T(8,128)S(1)}) custom-call(s32[64]{0:T(128)S(1)} %copy-done.2, s32[8]{0:T(128)S(1)} %copy-done.3, bf16[8,256,1024]{2,1,0:T(8,128)(2,1)S(1)} %bitcast.13, f32[16,128]{1,0:T(8,128)S(1)} %bitcast.17, ...), custom_call_target="tpu_custom_call" | custom-call | tf_op jit(solution)/shard_map/scores/pallas_call | solution.py:229
  134.4 11.7 %all_to_all.32.got_ref = f32[16,32,128]{2,1,0:T(8,128)S(1)} all-to-all(f32[16,32,128]{2,1,0:T(8,128)S(1)} %get-tuple-element.23), channel_id=1, replica_groups=mesh['rows'=16,'cents'=8] {'rows'}, dimensions={0} | all-to-all | bytes 524288 | tf_op jit(solution)/shard_map/all_to_all | solution.py:489
  146.1 1.9 turn.2
  148.0 11.6 %all_to_all.33.got_ref = f32[16,32,128]{2,1,0:T(8,128)S(1)} all-to-all(f32[16,32,128]{2,1,0:T(8,128)S(1)} %turn.2), channel_id=1, replica_groups=mesh['rows'=16,'cents'=8] {'rows'}, dimensions={0} | all-to-all | bytes 524288 | tf_op jit(solution)/shard_map/all_to_all | solution.py:489
  159.6 1.9 turn.3
  161.6 11.6 %all_to_all.34.got_ref = f32[16,32,128]{2,1,0:T(8,128)S(1)} all-to-all(f32[16,32,128]{2,1,0:T(8,128)S(1)} %turn.3), channel_id=1, replica_groups=mesh['rows'=16,'cents'=8] {'rows'}, dimensions={0} | all-to-all | bytes 524288 | tf_op jit(solution)/shard_map/all_to_all | solution.py:489
  173.2 11.0 %final_pass.1 = bf16[16,2064,128]{2,1,0:T(8,128)(2,1)S(1)} custom-call(s32[64]{0:T(128)S(1)} %copy-done.2, f32[8,8,256,128]{3,2,1,0:T(8,128)S(1)} %get-tuple-element.20.kernel_ref, f32[8,256,128]{2,1,0:T(8,128)S(1)} %get-tuple-element.21.weight_ref, bf16[8,256,1024]{2,1,0:T(8,128)(2,1)S(1)} %get-tuple-element.22.rows_ref, ...), custom_call_target="tpu_custom_call" | custom-call | tf_op jit(solution)/shard_map/final_pass/pallas_call | solution.py:379
  184.1 96.9 %all_to_all.35.got_ref = bf16[16,2064,128]{2,1,0:T(8,128)(2,1)S(1)} all-to-all(bf16[16,2064,128]{2,1,0:T(8,128)(2,1)S(1)} %final_pass.1), channel_id=1, replica_groups=mesh['rows'=16,'cents'=8] {'rows'}, dimensions={0} | all-to-all | bytes 16908288 | tf_op jit(solution)/shard_map/all_to_all | solution.py:489
  281.0 6.1 %merge.1 = (f32[16,128,1024]{2,1,0:T(8,128)}, f32[16,128]{1,0:T(8,128)}) custom-call(s32[32]{0:T(128)S(1)} %get-tuple-element.17.wanted_ref, bf16[16,2064,128]{2,1,0:T(8,128)(2,1)S(1)} %all_to_all.35.got_ref, f32[8,128]{1,0:T(8,128)S(1)} %get-tuple-element.25.target_ref), custom_call_target="tpu_custom_call" | custom-call | tf_op jit(solution)/shard_map/merge/pallas_call | solution.py:468
Async XLA Ops:
  28.3 99.0 %copy-start = (bf16[2048,1024]{1,0:T(8,128)(2,1)S(1)}, bf16[2048,1024]{1,0:T(8,128)(2,1)}, u32[]{:S(2)}) copy-start(bf16[2048,1024]{1,0:T(8,128)(2,1)} %param.5) | copy-start | bytes 12582916
  28.3 99.0 %copy-start.1 = (f32[2048]{0:T(1024)S(1)}, f32[2048]{0:T(1024)}, u32[]{:S(2)}) copy-start(f32[2048]{0:T(1024)} %param.7) | copy-start | bytes 24580
  28.3 99.0 %copy-start.2 = (s32[64]{0:T(128)S(1)}, s32[64]{0:T(128)}, u32[]{:S(2)}) copy-start(s32[64]{0:T(128)} %get-tuple-element.18.dist_ref) | copy-start | bytes 772
  28.3 99.0 %copy-start.3 = (s32[8]{0:T(128)S(1)}, s32[8]{0:T(128)}, u32[]{:S(2)}) copy-start(s32[8]{0:T(128)} %count_ref.1) | copy-start | bytes 100
